TPU v7x, 1024 devices: a whole 8x8x8 slice. The times are simulated.
1024 devices in a mesh: grp: 32 (over y_lo, z), inner: 32 (over y_hi, x, core).
Axes of the slice: x: 8, y: 8 (y_hi: 2, y_lo: 4; y = y_hi * 4 + y_lo), z: 8, core: 2. Of those that a mesh axis runs over, the one named last changes fastest.
Arguments:
- b_tensor: bfloat16 [10, 8192, 3072], P(None, ('grp', 'inner')), may hold values from -0.59765625 to 0.59765625
- occ_energy: float32 [10], replicated, may hold values from -2 to -0.5
- vir_energy: float32 [3072], replicated, may hold values from 0.5 to 4
- left_list: int32 [3], replicated, may hold values from 0 to 9
- right_occ: int32 [1], replicated, may hold values from 0 to 9
Outputs:
- gamma_aux: float32 [10, 8192, 3072], P(None, ('grp', 'inner'))
Inputs may be any that keep to these rules, and one draw needn't show every extreme that they name: `left_list`: each entry is an occupied orbital of the window; a first orbital may equal the second, and first orbitals may repeat. `right_occ`: an occupied orbital of the window.
All inputs are finite; a program needn't handle non-finite values.
Results may differ from a plain program's by a relative error of at most 0.0023.
Values may be sent and summed in bfloat16 or wider, within the bound.
No kernel may reach another device: no remote copies, remote signals or barrier semaphores. Data moves between devices by JAX's collectives and lax.ppermute only.
A program may use at most 32 MiB of HBM per device.

v0:
```python
import jax
import jax.numpy as jnp
from jax import lax
from jax.sharding import PartitionSpec as P


def body(b_tensor, occ_energy, vir_energy, left_list, right_occ):
    inner_size = lax.axis_size("inner")
    group_size = lax.axis_size("grp")
    occ_count = b_tensor.shape[0]
    virtuals = b_tensor.shape[2]
    row_count = virtuals // inner_size
    col_count = virtuals // group_size
    inner_rank = lax.axis_index("inner")
    group_rank = lax.axis_index("grp")
    vir_rows = lax.dynamic_slice_in_dim(vir_energy, inner_rank * row_count, row_count)
    vir_cols = lax.dynamic_slice_in_dim(vir_energy, group_rank * col_count, col_count)
    gamma_aux = jnp.zeros(b_tensor.shape, jnp.float32)
    orbitals = jnp.arange(occ_count, dtype=jnp.int32)
    second_occ = right_occ[0]
    block_right = lax.dynamic_index_in_dim(b_tensor, second_occ, 0, keepdims=False)
    right_full = lax.all_gather(block_right, "inner", axis=0, tiled=True)
    pair_total = left_list.shape[0]
    selectors = []
    amp_list = []
    for pair_no in range(pair_total):
        left_occ = left_list[pair_no]
        block_left = lax.dynamic_index_in_dim(b_tensor, left_occ, 0, keepdims=False)
        left_rows = lax.all_to_all(block_left, "inner", split_axis=1, concat_axis=0, tiled=True)
        partial_value = lax.dot_general(
            left_rows, right_full, (((0,), (0,)), ((), ())), preferred_element_type=jnp.float32
        )
        shift_occ = occ_energy[left_occ] + occ_energy[second_occ]
        selectors.append((orbitals == left_occ).astype(jnp.float32))
        shares = lax.psum_scatter(partial_value, "grp", scatter_dimension=1, tiled=True)
        denominator = shift_occ - vir_rows[:, None] - vir_cols[None, :]
        amp_tile = (shares / denominator).astype(jnp.bfloat16)
        amp_list.append(lax.all_gather(amp_tile, "grp", axis=1, tiled=True))
    for pair_no in range(pair_total):
        contrib = lax.dot_general(
            right_full,
            amp_list[pair_no],
            (((1,), (1,)), ((), ())),
            preferred_element_type=jnp.float32,
        )
        returned = lax.all_to_all(contrib, "inner", split_axis=0, concat_axis=1, tiled=True)
        gamma_aux = gamma_aux + selectors[pair_no][:, None, None] * returned[None]
    return gamma_aux


def solution(mesh):
    placed = (P(None, ("grp", "inner"), None), P(), P(), P(), P())
    return jax.shard_map(
        body, mesh=mesh, in_specs=placed, out_specs=P(None, ("grp", "inner"), None), check_vma=False
    )
```

profile of v0, /device:TPU:1, one launch (start us, length us, event | category | flops | bytes accessed | tf_op | source)
XLA Modules:
  0.0 917.2 jit_solution(16995418256491678010)
XLA Ops:
  6.5 0.0 all-gather.3.cloned.1.call-start
  6.5 1.4 fusion.22
  14.2 1.5 constant_dynamic-slice_fusion.2
  15.8 0.0 all-gather.3.cloned.1.call-update
  15.8 0.0 reduce-scatter.12.cloned.1.call-start
  15.8 0.1 all_to_all.85
  16.0 28.8 %all_to_all.105 = bf16[8,32,96]{2,0,1:T(8,128)(2,1)S(1)} all-to-all(bf16[8,32,96]{2,0,1:T(8,128)(2,1)S(1)} %copy.25), channel_id=1, replica_groups=mesh['grp'=32,'inner'=32] {'inner'}, dimensions={1} | all-to-all | bytes 98304 | tf_op jit(solution)/shard_map/all_to_all | solution.py:29
  44.9 79.9 %all-gather.3.cloned.1.call-done = bf16[1,256,3072]{2,1,0:T(8,128)(2,1)} async-done(((bf16[1,8,3072]{2,1,0:T(8,128)(2,1)}), bf16[1,256,3072]{2,1,0:T(8,128)(2,1)}) %all-gather.3.cloned.1.call-update) | async-done | bytes 1572880 | tf_op jit(solution)/shard_map/all_gather | solution.py:22
  124.8 3.3 convolution_bitcast_fusion.1
  128.1 0.0 copy-start
  128.1 0.0 reduce-scatter.12.cloned.1.call-update
  128.1 0.0 reduce-scatter.14.cloned.1.call-start
  128.2 0.1 all_to_all.92
  128.4 16.3 %all_to_all.106 = bf16[8,32,96]{2,0,1:T(8,128)(2,1)S(1)} all-to-all(bf16[8,32,96]{2,0,1:T(8,128)(2,1)S(1)} %copy.29), channel_id=1, replica_groups=mesh['grp'=32,'inner'=32] {'inner'}, dimensions={1} | all-to-all | bytes 98304 | tf_op jit(solution)/shard_map/all_to_all | solution.py:29
  144.7 0.0 copy-done
  144.7 1.9 convolution_bitcast_fusion
  146.6 0.0 reduce-scatter.14.cloned.1.call-update
  146.6 0.0 reduce-scatter.10.cloned.1.call-start
  146.7 0.1 all_to_all.78
  146.8 15.9 %all_to_all.107 = bf16[8,32,96]{2,0,1:T(8,128)(2,1)S(1)} all-to-all(bf16[8,32,96]{2,0,1:T(8,128)(2,1)S(1)} %copy.21), channel_id=1, replica_groups=mesh['grp'=32,'inner'=32] {'inner'}, dimensions={1} | all-to-all | bytes 98304 | tf_op jit(solution)/shard_map/all_to_all | solution.py:29
  162.8 1.9 convolution_bitcast_fusion.2
  164.7 0.0 copy-start.1
  164.7 0.0 reduce-scatter.10.cloned.1.call-update
  164.7 0.6 copy-done.1
  165.3 0.7 fusion.21
  169.8 0.9 broadcast_subtract_fusion.2
  170.6 95.8 %reduce-scatter.12.cloned.1.call-done = f32[96,96]{1,0:T(8,128)} async-done(((f32[3072,96]{1,0:T(8,128)}), f32[96,96]{1,0:T(8,128)}) %reduce-scatter.12.cloned.1.call-update) | async-done | bytes 36880
  266.5 0.9 copy.39
  267.3 163.4 %reduce-scatter.14.cloned.1.call-done = f32[96,96]{1,0:T(8,128)} async-done(((f32[3072,96]{1,0:T(8,128)}), f32[96,96]{1,0:T(8,128)}) %reduce-scatter.14.cloned.1.call-update) | async-done | bytes 36880
  430.7 0.9 copy.41
  431.6 162.9 %reduce-scatter.10.cloned.1.call-done = f32[96,96]{1,0:T(8,128)} async-done(((f32[3072,96]{1,0:T(8,128)}), f32[96,96]{1,0:T(8,128)}) %reduce-scatter.10.cloned.1.call-update) | async-done | bytes 36880
  594.4 0.9 copy.37
  595.3 0.1 divide_convert_fusion.2
  595.4 0.1 copy.22
  595.6 64.5 %all_gather.13 = bf16[96,3072]{0,1:T(8,128)(2,1)S(1)} all-gather(bf16[96,96]{0,1:T(8,128)(2,1)S(1)} %copy.22), channel_id=1, replica_groups=mesh['grp'=32,'inner'=32] {'grp'}, dimensions={1}, use_global_device_ids=true | all-gather | bytes 608256 | tf_op jit(solution)/shard_map/all_gather | solution.py:38
  660.1 1.2 fusion.9
  661.3 46.9 %all-to-all-start.1 = ((f32[32,8,96]{2,1,0:T(8,128)}), f32[32,8,96]{2,1,0:T(8,128)S(1)}, u32[]{:S(2)}, u32[]{:S(2)}) async-start(f32[32,8,96]{2,1,0:T(8,128)} %fusion.9), calls=%async_computation.1 | async-start | bytes 262144 | tf_op jit(solution)/shard_map/all_to_all | solution.py:46
  708.2 0.1 copy.26
  708.3 65.2 %all_gather.14 = bf16[96,3072]{0,1:T(8,128)(2,1)S(1)} all-gather(bf16[96,96]{0,1:T(8,128)(2,1)S(1)} %copy.26), channel_id=1, replica_groups=mesh['grp'=32,'inner'=32] {'grp'}, dimensions={1}, use_global_device_ids=true | all-gather | bytes 608256 | tf_op jit(solution)/shard_map/all_gather | solution.py:38
  773.5 0.1 copy.30
  773.6 64.5 %all_gather.15 = bf16[96,3072]{0,1:T(8,128)(2,1)S(1)} all-gather(bf16[96,96]{0,1:T(8,128)(2,1)S(1)} %copy.30), channel_id=1, replica_groups=mesh['grp'=32,'inner'=32] {'grp'}, dimensions={1}, use_global_device_ids=true | all-gather | bytes 608256 | tf_op jit(solution)/shard_map/all_gather | solution.py:38
  838.0 1.2 fusion.12
  839.2 0.0 all-to-all-done.1
  839.2 38.9 %all-to-all-start.3 = ((f32[32,8,96]{2,1,0:T(8,128)}), f32[32,8,96]{2,1,0:T(8,128)S(1)}, u32[]{:S(2)}, u32[]{:S(2)}) async-start(f32[32,8,96]{2,1,0:T(8,128)} %fusion.12), calls=%async_computation.3 | async-start | bytes 262144 | tf_op jit(solution)/shard_map/all_to_all | solution.py:46
  878.2 1.2 fusion.15
  879.4 11.8 %all-to-all-done.3 = f32[32,8,96]{2,1,0:T(8,128)S(1)} async-done(((f32[32,8,96]{2,1,0:T(8,128)}), f32[32,8,96]{2,1,0:T(8,128)S(1)}, u32[]{:S(2)}, u32[]{:S(2)}) %all-to-all-start.3) | async-done | bytes 98336 | tf_op jit(solution)/shard_map/all_to_all | solution.py:46
  891.1 5.1 all-to-all-start.5
  896.3 0.6 compare_convert_fusion.2
  896.9 1.3 compare_convert_fusion
  898.2 0.1 mul.54
  898.4 0.1 mul.58
  898.5 10.9 %all-to-all-done.5 = f32[32,8,96]{2,1,0:T(8,128)S(1)} async-done(((f32[32,8,96]{2,1,0:T(8,128)}), f32[32,8,96]{2,1,0:T(8,128)S(1)}, u32[]{:S(2)}, u32[]{:S(2)}) %all-to-all-start.5) | async-done | bytes 98336 | tf_op jit(solution)/shard_map/all_to_all | solution.py:46
  909.4 0.1 mul.62
  909.5 1.2 multiply_add_fusion
  (6 shorter events, 0.2 us)
Async XLA Ops:
  6.5 118.3 %all-gather.3.cloned.1.call-start = ((), (), s32[]{:S(2)}) async-start(), calls=%async_computation.9 | async-start | bytes 1622016 | tf_op jit(solution)/shard_map/all_gather | solution.py:22
  15.8 250.7 %reduce-scatter.12.cloned.1.call-start = ((), (), s32[]{:S(2)}) async-start(), calls=%async_computation.11 | async-start | bytes 1622016
  128.1 16.6 %copy-start = (bf16[1,256,3072]{2,1,0:T(8,128)(2,1)S(1)}, bf16[1,256,3072]{2,1,0:T(8,128)(2,1)}, u32[]{:S(2)}) copy-start(bf16[1,256,3072]{2,1,0:T(8,128)(2,1)} %all-gather.3.cloned.1.call-done) | copy-start | bytes 4718596
  128.1 302.6 %reduce-scatter.14.cloned.1.call-start = ((), (), s32[]{:S(2)}) async-start(), calls=%async_computation.12 | async-start | bytes 1622016
  146.6 447.8 %reduce-scatter.10.cloned.1.call-start = ((), (), s32[]{:S(2)}) async-start(), calls=%async_computation.10 | async-start | bytes 1622016
  164.7 0.7 copy-start.1
  661.3 177.9 %all-to-all-start.1 = ((f32[32,8,96]{2,1,0:T(8,128)}), f32[32,8,96]{2,1,0:T(8,128)S(1)}, u32[]{:S(2)}, u32[]{:S(2)}) async-start(f32[32,8,96]{2,1,0:T(8,128)} %fusion.9), calls=%async_computation.1 | async-start | bytes 262144 | tf_op jit(solution)/shard_map/all_to_all | solution.py:46
  839.2 51.9 %all-to-all-start.3 = ((f32[32,8,96]{2,1,0:T(8,128)}), f32[32,8,96]{2,1,0:T(8,128)S(1)}, u32[]{:S(2)}, u32[]{:S(2)}) async-start(f32[32,8,96]{2,1,0:T(8,128)} %fusion.12), calls=%async_computation.3 | async-start | bytes 262144 | tf_op jit(solution)/shard_map/all_to_all | solution.py:46
  891.1 18.2 %all-to-all-start.5 = ((f32[32,8,96]{2,1,0:T(8,128)}), f32[32,8,96]{2,1,0:T(8,128)S(1)}, u32[]{:S(2)}, u32[]{:S(2)}) async-start(f32[32,8,96]{2,1,0:T(8,128)} %fusion.15), calls=%async_computation.5 | async-start | bytes 262144 | tf_op jit(solution)/shard_map/all_to_all | solution.py:46
Sparse Core Ops, SparseCore 0:
  15.9 108.8 all-gather.2
  128.3 138.1 reduce-scatter.11
  270.2 160.4 reduce-scatter.13
  433.9 160.4 reduce-scatter.9
where the time goes:
time: 918 us; the launch traced here: 917 us
  waiting for transfers between devices  525 us (57%)
  blocking collectives  255 us (28%)
  starting transfers between devices  91.1 us (10%)
  between operations  23.4 us (3%)
  matrix products  10.8 us (1%)
    unnamed x7, waiting for transfers between devices  422 us
    all_gather x3, blocking collectives, body(): amp_list.append(lax.all_gather(amp_tile, 'grp', axis=1, tiled=True))  194 us
    all_to_all x3, starting transfers between devices, body(): lax.all_to_all(contrib, 'inner', split_axis=0, concat_axis=1, tiled=True)  90.9 us
    all_gather x1, waiting for transfers between devices, body(): right_full = lax.all_gather(block_right, 'inner', axis=0, tiled=True)  79.9 us
    all_to_all x3, blocking collectives, body(): lax.all_to_all(block_left, 'inner', split_axis=1, concat_axis=0, tiled=True)  61.1 us
    all_to_all x3, waiting for transfers between devices, body(): lax.all_to_all(contrib, 'inner', split_axis=0, concat_axis=1, tiled=True)  22.6 us
  transfers between devices with their start and end apart: 7, of which 6 were waited for; matrix products, arithmetic and copies ran while one was open for 1% of the time, Pallas kernels for 0%

commit v1 on v0

v1 whole, which is shorter than its diff:
```python
import jax
import jax.numpy as jnp
import numpy as np
from jax import lax
from jax.sharding import Mesh, PartitionSpec as P

GRP_BITS = ("y1", "y0", "z2", "z1", "z0")
INNER_BITS = ("y2", "x2", "x1", "x0", "c")
ALL_BITS = GRP_BITS + INNER_BITS
A_BITS = ("x2", "x1", "y2", "y1")
B_BITS = ("z2", "z1")
AB_BITS = A_BITS + B_BITS
B_SUM_BITS = ("c",)
A_SUM_BITS = ("x0", "y0", "z0")
SUM_BITS = B_SUM_BITS + A_SUM_BITS


def exchange(x, axes):
    return lax.all_to_all(x, axes, split_axis=0, concat_axis=0, tiled=True)


def body(b_tensor, occ_energy, vir_energy, left_list, right_occ):
    occ_count, rows, virtuals = b_tensor.shape
    pairs = left_list.shape[0]
    a_parts, b_parts = 2 ** len(A_BITS), 2 ** len(B_BITS)
    a_subs, b_subs = 2 ** len(A_SUM_BITS), 2 ** len(B_SUM_BITS)
    a_width, b_width = virtuals // a_parts, virtuals // b_parts
    pa_width = pairs * a_width
    sub_rows, sub_cols = pa_width // a_subs, b_width // b_subs
    peers, subs = a_parts * b_parts, a_subs * b_subs
    group_rows = peers * rows

    second_occ = right_occ[0]
    block_right = lax.dynamic_index_in_dim(b_tensor, second_occ, 0, keepdims=False)
    block_left = jnp.stack(
        [lax.dynamic_index_in_dim(b_tensor, left_list[p], 0, keepdims=False) for p in range(pairs)]
    )

    to_b = block_right.reshape(rows, b_parts, b_width).transpose(1, 0, 2)
    to_a = block_left.reshape(pairs, rows, a_parts, a_width).transpose(2, 1, 0, 3).reshape(a_parts, rows, pa_width)
    packed = jnp.concatenate(
        [
            jnp.broadcast_to(to_b[None], (a_parts, b_parts, rows, b_width)),
            jnp.broadcast_to(to_a[:, None], (a_parts, b_parts, rows, pa_width)),
        ],
        axis=-1,
    )
    got = exchange(packed.reshape(peers, rows, b_width + pa_width), AB_BITS)
    got = got.reshape(group_rows, b_width + pa_width)
    right = got[:, :b_width].reshape(group_rows, b_subs, sub_cols)
    left = got[:, b_width:]

    partial_value = lax.dot_general(left, right, (((0,), (0,)), ((), ())), preferred_element_type=jnp.float32)
    partial_value = partial_value.transpose(1, 0, 2).reshape(subs, sub_rows, sub_cols)
    shares = exchange(partial_value, SUM_BITS).sum(axis=0)

    a_rank, b_rank = lax.axis_index(A_BITS), lax.axis_index(B_BITS)
    a_sub, b_sub = lax.axis_index(A_SUM_BITS), lax.axis_index(B_SUM_BITS)
    vir_a = lax.dynamic_slice_in_dim(vir_energy, a_rank * a_width, a_width)
    shift = occ_energy[left_list] + occ_energy[second_occ]
    row_part = (shift[:, None] - vir_a[None, :]).reshape(pa_width)
    row_part = lax.dynamic_slice_in_dim(row_part, a_sub * sub_rows, sub_rows)
    vir_b = lax.dynamic_slice_in_dim(vir_energy, b_rank * b_width + b_sub * sub_cols, sub_cols)
    denominator = row_part[:, None] - vir_b[None, :]
    amp_tile = (shares / denominator).astype(jnp.bfloat16)

    amps = exchange(jnp.broadcast_to(amp_tile[None], (subs, sub_rows, sub_cols)), SUM_BITS)
    amps = amps.reshape(b_subs, pa_width, sub_cols)
    contrib = lax.dot_general(right, amps, (((1, 2), (0, 2)), ((), ())), preferred_element_type=jnp.float32)
    returned = exchange(contrib.reshape(peers, rows, pa_width), AB_BITS)
    returned = returned.reshape(a_parts, b_parts, rows, pairs, a_width).sum(axis=1)
    returned = returned.transpose(2, 1, 0, 3).reshape(pairs, rows, virtuals)

    orbitals = jnp.arange(occ_count, dtype=jnp.int32)
    gamma_aux = jnp.zeros(b_tensor.shape, jnp.float32)
    for p in range(pairs):
        chosen = (orbitals == left_list[p]).astype(jnp.float32)
        gamma_aux = gamma_aux + chosen[:, None, None] * returned[p][None]
    return gamma_aux


def solution(mesh):
    fine = Mesh(np.asarray(mesh.devices).reshape((2,) * len(ALL_BITS)), ALL_BITS)
    placed = (P(None, ALL_BITS, None), P(), P(), P(), P())
    return jax.shard_map(body, mesh=fine, in_specs=placed, out_specs=P(None, ALL_BITS, None), check_vma=False)
```

time: 918 us -> 197 us (0.21)
  the two profiles are of different devices: /device:TPU:1 before, /device:TPU:82 now
where the time goes in v1:
time: 197 us
  blocking collectives  80.7 us (41%)
  waiting for transfers between devices  67.1 us (34%)
  starting transfers between devices  25 us (13%)
  local copies, waits for them, and re-layouts  8.05 us (4%)
  between operations  6.83 us (3%)
  other arithmetic  4.97 us (3%)
  matrix products  3.91 us (2%)
    all_to_all x2, blocking collectives, exchange(): return lax.all_to_all(x, axes, split_axis=0, concat_axis=0, tiled=True)  80.7 us
    all_to_all x2, waiting for transfers between devices, exchange(): return lax.all_to_all(x, axes, split_axis=0, concat_axis=0, tiled=True)  67.1 us
    all_to_all x2, starting transfers between devices, exchange(): return lax.all_to_all(x, axes, split_axis=0, concat_axis=0, tiled=True)  25 us
  transfers between devices with their start and end apart: 2, of which 2 were waited for; matrix products, arithmetic and copies ran while one was open for 3% of the time, Pallas kernels for 0%

profile of v1, /device:TPU:82, one launch (start us, length us, event | category | flops | bytes accessed | tf_op | source)
XLA Modules:
  0.0 196.6 jit_solution(14360384635303038938)
XLA Ops:
  0.0 1.4 fusion.2
  8.1 0.9 constant_dynamic-slice_fusion.3
  9.0 0.2 reshape.92
  9.2 0.2 copy.32
  9.4 0.2 broadcast_in_dim.11
  9.7 0.1 broadcast_in_dim.12
  9.7 0.1 broadcast_in_dim.10
  9.8 0.1 pad_maximum_fusion
  9.9 63.2 %all_to_all.20 = bf16[64,8,1344]{2,1,0:T(8,128)(2,1)S(1)} all-to-all(bf16[64,8,1344]{2,1,0:T(8,128)(2,1)S(1)} %bitcast.41), channel_id=1, replica_groups=mesh['y1'=2,'y0'=2,'z2'=2,'z1'=2,'z0'=2,'y2'=2,'x2'=2,'x1'=2,'x0'=2,'c'=..., dimensions={0} | all-to-all | bytes 2752512 | tf_op jit(solution)/shard_map/all_to_all | solution.py:19
  73.1 0.1 slice.40
  73.2 0.3 copy.22
  73.5 2.0 %fusion = f32[576,2,384]{2,0,1:T(8,128)} fusion(bf16[512,2,384]{0,2,1:T(8,128)(2,1)S(1)} %bitcast.43, bf16[512,1344]{1,0:T(8,128)(2,1)S(1)} %bitcast.40), kind=kOutput, calls=%fused_computation.5 | convolution fusion | flops 452984832 | bytes 3211264 | tf_op jit(solution)/shard_map/dot_general | solution.py:53
  75.5 0.0 copy-start
  75.5 0.0 copy-start.1
  75.5 10.0 %all-to-all-start.1 = ((f32[16,72,384]{2,1,0:T(8,128)}), f32[16,72,384]{2,1,0:T(8,128)S(1)}, u32[]{:S(2)}, u32[]{:S(2)}) async-start(f32[16,72,384]{2,1,0:T(8,128)} %bitcast.12), calls=%async_computation.1 | async-start | bytes 3538944 | tf_op jit(solution)/shard_map/all_to_all | solution.py:19
  85.6 0.0 copy-done
  85.6 0.6 dynamic_slice.29
  86.2 0.0 copy-done.1
  86.2 0.6 gather_fusion
  86.8 0.8 dynamic_slice.30
  87.6 0.6 broadcast_add_fusion
  88.2 0.1 broadcast_subtract_fusion
  88.3 0.1 sub.37
  88.4 0.8 dynamic_slice.32
  89.2 0.1 dynamic_slice.31
  89.2 19.8 %all-to-all-done.1 = f32[16,72,384]{2,1,0:T(8,128)S(1)} async-done(((f32[16,72,384]{2,1,0:T(8,128)}), f32[16,72,384]{2,1,0:T(8,128)S(1)}, u32[]{:S(2)}, u32[]{:S(2)}) %all-to-all-start.1) | async-done | bytes 1769504 | tf_op jit(solution)/shard_map/all_to_all | solution.py:19
  109.0 0.1 reduce_sum.18
  109.1 0.1 divide_convert_fusion
  109.2 0.1 broadcast_in_dim.14
  109.3 17.5 %all_to_all.21 = bf16[16,72,384]{2,1,0:T(8,128)(2,1)S(1)} all-to-all(bf16[16,72,384]{2,1,0:T(8,128)(2,1)S(1)} %broadcast_in_dim.14), channel_id=1, replica_groups=mesh['y1'=2,'y0'=2,'z2'=2,'z1'=2,'z0'=2,'y2'=2,'x2'=2,'x1'=2,'x0'=2,'c'=..., dimensions={0} | all-to-all | bytes 1769472 | tf_op jit(solution)/shard_map/all_to_all | solution.py:19
  126.8 1.9 convolution_bitcast_fusion
  128.7 14.9 %all-to-all-start.3 = ((f32[64,8,576]{2,1,0:T(8,128)}), f32[64,8,576]{2,1,0:T(8,128)S(1)}, u32[]{:S(2)}, u32[]{:S(2)}) async-start(f32[64,8,576]{2,1,0:T(8,128)} %convolution_bitcast_fusion), calls=%async_computation.3 | async-start | bytes 2621440 | tf_op jit(solution)/shard_map/all_to_all | solution.py:19
  143.7 0.7 compare_convert_fusion.2
  144.4 1.3 compare_convert_fusion
  145.7 47.3 %all-to-all-done.3 = f32[64,8,576]{2,1,0:T(8,128)S(1)} async-done(((f32[64,8,576]{2,1,0:T(8,128)}), f32[64,8,576]{2,1,0:T(8,128)S(1)}, u32[]{:S(2)}, u32[]{:S(2)}) %all-to-all-start.3) | async-done | bytes 1179680 | tf_op jit(solution)/shard_map/all_to_all | solution.py:19
  193.0 0.9 reshape.98
  193.9 0.7 reduce_sum.19
  194.6 0.3 fusion.1
  195.0 0.1 mul.86
  195.1 0.1 mul.90
  195.3 0.1 mul.94
  195.4 1.2 multiply_add_fusion
  (8 shorter events, 0.2 us)
Async XLA Ops:
  75.5 10.1 %copy-start = (f32[10]{0:T(128)S(1)}, f32[10]{0:T(128)}, u32[]{:S(2)}) copy-start(f32[10]{0:T(128)} %param.6) | copy-start | bytes 124
  75.5 10.6 %copy-start.1 = (s32[3]{0:T(128)S(1)}, s32[3]{0:T(128)}, u32[]{:S(2)}) copy-start(s32[3]{0:T(128)} %param.8) | copy-start | bytes 40
  75.5 33.5 %all-to-all-start.1 = ((f32[16,72,384]{2,1,0:T(8,128)}), f32[16,72,384]{2,1,0:T(8,128)S(1)}, u32[]{:S(2)}, u32[]{:S(2)}) async-start(f32[16,72,384]{2,1,0:T(8,128)} %bitcast.12), calls=%async_computation.1 | async-start | bytes 3538944 | tf_op jit(solution)/shard_map/all_to_all | solution.py:19
  128.7 64.3 %all-to-all-start.3 = ((f32[64,8,576]{2,1,0:T(8,128)}), f32[64,8,576]{2,1,0:T(8,128)S(1)}, u32[]{:S(2)}, u32[]{:S(2)}) async-start(f32[64,8,576]{2,1,0:T(8,128)} %convolution_bitcast_fusion), calls=%async_computation.3 | async-start | bytes 2621440 | tf_op jit(solution)/shard_map/all_to_all | solution.py:19

commit v2 on v1

v2 whole, which is shorter than its diff:
```python
import jax
import jax.numpy as jnp
import numpy as np
from jax import lax
from jax.experimental import pallas as pl
from jax.experimental.pallas import tpu as pltpu
from jax.sharding import Mesh, PartitionSpec as P

GRP_BITS = ("y1", "y0", "z2", "z1", "z0")
INNER_BITS = ("y2", "x2", "x1", "x0", "c")
ALL_BITS = GRP_BITS + INNER_BITS
A_BITS = ("x2", "x1", "y2", "y1")
B_BITS = ("z2", "z1")
AB_BITS = A_BITS + B_BITS
B_SUM_BITS = ("c",)
A_SUM_BITS = ("x0", "y0", "z0")
SUM_BITS = B_SUM_BITS + A_SUM_BITS
INTERPRET = False


def exchange(x, axes):
    return lax.all_to_all(x, axes, split_axis=0, concat_axis=0, tiled=True)


def pack_rows(left_list, right_occ, b_tensor, a_parts, b_parts):
    _, rows, virtuals = b_tensor.shape
    pairs = left_list.shape[0]
    a_width, b_width = virtuals // a_parts, virtuals // b_parts

    def kernel(left_ref, right_ref, b_ref, out_ref, buf, sems):
        copies = []
        for p in range(pairs + 1):
            orbital = right_ref[0] if p == pairs else left_ref[p]
            copies.append(pltpu.make_async_copy(b_ref.at[orbital], buf.at[p], sems.at[p]))
            copies[-1].start()
        for p in range(pairs):
            copies[p].wait()
            start = b_width + p * a_width
            for a in range(a_parts):
                piece = buf[p, :, a * a_width : (a + 1) * a_width]
                for b in range(b_parts):
                    out_ref[a * b_parts + b, :, start : start + a_width] = piece
        copies[pairs].wait()
        for b in range(b_parts):
            piece = buf[pairs, :, b * b_width : (b + 1) * b_width]
            for a in range(a_parts):
                out_ref[a * b_parts + b, :, :b_width] = piece

    return pl.pallas_call(
        kernel,
        out_shape=jax.ShapeDtypeStruct((a_parts * b_parts, rows, b_width + pairs * a_width), b_tensor.dtype),
        in_specs=[
            pl.BlockSpec(memory_space=pltpu.SMEM),
            pl.BlockSpec(memory_space=pltpu.SMEM),
            pl.BlockSpec(memory_space=pl.ANY),
        ],
        out_specs=pl.BlockSpec(memory_space=pltpu.VMEM),
        scratch_shapes=[pltpu.VMEM((pairs + 1, rows, virtuals), b_tensor.dtype), pltpu.SemaphoreType.DMA((pairs + 1,))],
        interpret=INTERPRET,
    )(left_list, right_occ, b_tensor)


def place_rows(left_list, returned, occ_count, a_parts, b_parts):
    _, rows, pa_width = returned.shape
    pairs = left_list.shape[0]
    a_width = pa_width // pairs
    virtuals = a_parts * a_width

    def kernel(left_ref, in_ref, out_ref, rows_ref):
        for a in range(a_parts):
            total = in_ref[a * b_parts].astype(jnp.float32)
            for b in range(1, b_parts):
                total = total + in_ref[a * b_parts + b].astype(jnp.float32)
            for p in range(pairs):
                rows_ref[p, :, a * a_width : (a + 1) * a_width] = total[:, p * a_width : (p + 1) * a_width]
        for orbital in range(occ_count):
            total = jnp.zeros((rows, virtuals), jnp.float32)
            for p in range(pairs):
                total = total + jnp.where(left_ref[p] == orbital, rows_ref[p], 0.0)
            out_ref[orbital] = total

    return pl.pallas_call(
        kernel,
        out_shape=jax.ShapeDtypeStruct((occ_count, rows, virtuals), jnp.float32),
        in_specs=[pl.BlockSpec(memory_space=pltpu.SMEM), pl.BlockSpec(memory_space=pltpu.VMEM)],
        out_specs=pl.BlockSpec(memory_space=pltpu.VMEM),
        scratch_shapes=[pltpu.VMEM((pairs, rows, virtuals), jnp.float32)],
        interpret=INTERPRET,
    )(left_list, returned)


def body(b_tensor, occ_energy, vir_energy, left_list, right_occ):
    occ_count, rows, virtuals = b_tensor.shape
    pairs = left_list.shape[0]
    a_parts, b_parts = 2 ** len(A_BITS), 2 ** len(B_BITS)
    a_subs, b_subs = 2 ** len(A_SUM_BITS), 2 ** len(B_SUM_BITS)
    a_width, b_width = virtuals // a_parts, virtuals // b_parts
    pa_width = pairs * a_width
    sub_rows, sub_cols = pa_width // a_subs, b_width // b_subs
    peers, subs = a_parts * b_parts, a_subs * b_subs
    group_rows = peers * rows

    second_occ = right_occ[0]
    packed = pack_rows(left_list, right_occ, b_tensor, a_parts, b_parts)
    got = exchange(packed, AB_BITS)
    got = got.reshape(group_rows, b_width + pa_width)
    right = got[:, :b_width]
    left = got[:, b_width:]

    b_sub = lax.axis_index(B_SUM_BITS)

    def partial_of(half):
        cols = lax.dynamic_slice_in_dim(right, half * sub_cols, sub_cols, axis=1)
        return lax.dot_general(left, cols, (((0,), (0,)), ((), ())), preferred_element_type=jnp.float32)

    received = lax.ppermute(partial_of(1 - b_sub), B_SUM_BITS, [(0, 1), (1, 0)])
    own = lax.optimization_barrier(partial_of(b_sub))
    paired = own + received
    shares = exchange(paired.reshape(a_subs, sub_rows, sub_cols), A_SUM_BITS).sum(axis=0)

    a_rank, b_rank = lax.axis_index(A_BITS), lax.axis_index(B_BITS)
    a_sub = lax.axis_index(A_SUM_BITS)
    vir_a = lax.dynamic_slice_in_dim(vir_energy, a_rank * a_width, a_width)
    shift = occ_energy[left_list] + occ_energy[second_occ]
    row_part = (shift[:, None] - vir_a[None, :]).reshape(pa_width)
    row_part = lax.dynamic_slice_in_dim(row_part, a_sub * sub_rows, sub_rows)
    vir_b = lax.dynamic_slice_in_dim(vir_energy, b_rank * b_width + b_sub * sub_cols, sub_cols)
    denominator = row_part[:, None] - vir_b[None, :]
    amp_tile = (shares / denominator).astype(jnp.bfloat16)

    amps = exchange(jnp.broadcast_to(amp_tile[None], (subs, sub_rows, sub_cols)), SUM_BITS)
    amps = amps.reshape(b_subs, pa_width, sub_cols)
    halves = right.reshape(group_rows, b_subs, sub_cols)
    contrib = lax.dot_general(halves, amps, (((1, 2), (0, 2)), ((), ())), preferred_element_type=jnp.float32)
    returned = exchange(contrib.reshape(peers, rows, pa_width).astype(jnp.bfloat16), AB_BITS)
    return place_rows(left_list, returned, occ_count, a_parts, b_parts)


def solution(mesh):
    fine = Mesh(np.asarray(mesh.devices).reshape((2,) * len(ALL_BITS)), ALL_BITS)
    placed = (P(None, ALL_BITS, None), P(), P(), P(), P())
    return jax.shard_map(body, mesh=fine, in_specs=placed, out_specs=P(None, ALL_BITS, None), check_vma=False)
```

time: 197 us -> 160 us (0.81)
  the two profiles are of different devices: /device:TPU:82 before, /device:TPU:2 now
where the time goes in v2:
time: 160 us; the launch traced here: 159 us
  blocking collectives  53.7 us (34%)
  waiting for transfers between devices  52.2 us (33%)
  starting transfers between devices  39.3 us (25%)
  Pallas kernels  5.29 us (3%)
  local copies, waits for them, and re-layouts  3.06 us (2%)
  other arithmetic  3 us (2%)
  matrix products  1.81 us (1%)
    all_to_all x2, blocking collectives, exchange(): return lax.all_to_all(x, axes, split_axis=0, concat_axis=0, tiled=True)  53.7 us
    all_to_all x2, waiting for transfers between devices, exchange(): return lax.all_to_all(x, axes, split_axis=0, concat_axis=0, tiled=True)  50.2 us
    all_to_all x2, starting transfers between devices, exchange(): return lax.all_to_all(x, axes, split_axis=0, concat_axis=0, tiled=True)  37.4 us
  transfers between devices with their start and end apart: 3, of which 3 were waited for; matrix products, arithmetic and copies ran while one was open for 3% of the time, Pallas kernels for 0%

profile of v2, /device:TPU:2, one launch (start us, length us, event | category | flops | bytes accessed | tf_op | source)
XLA Modules:
  0.0 159.1 jit_solution(8720674817794095158)
XLA Ops:
  0.7 2.9 %shard_map.55 = bf16[64,8,1344]{2,1,0:T(8,128)(2,1)} custom-call(s32[3]{0:T(128)} %left_ref.3, s32[1]{0:T(128)} %copy.7.right_ref, bf16[10,8,3072]{2,1,0:T(8,128)(2,1)} %b_ref.1), custom_call_target="tpu_custom_call" | custom-call | tf_op jit(solution)/shard_map/pallas_call | solution.py:49
  3.6 26.5 %all-to-all-start = ((bf16[64,8,1344]{2,1,0:T(8,128)(2,1)}), bf16[64,8,1344]{2,1,0:T(8,128)(2,1)S(1)}, u32[]{:S(2)}, u32[]{:S(2)}) async-start(bf16[64,8,1344]{2,1,0:T(8,128)(2,1)} %shard_map.55), calls=%async_computation | async-start | bytes 2883584 | tf_op jit(solution)/shard_map/all_to_all | solution.py:22
  30.1 41.1 %all-to-all-done = bf16[64,8,1344]{2,1,0:T(8,128)(2,1)S(1)} async-done(((bf16[64,8,1344]{2,1,0:T(8,128)(2,1)}), bf16[64,8,1344]{2,1,0:T(8,128)(2,1)S(1)}, u32[]{:S(2)}, u32[]{:S(2)}) %all-to-all-start) | async-done | bytes 1376288 | tf_op jit(solution)/shard_map/all_to_all | solution.py:22
  71.2 0.1 slice.10
  71.3 0.5 fusion.1
  71.8 1.9 %collective-permute-start = (f32[576,384]{1,0:T(8,128)S(1)}, f32[576,384]{1,0:T(8,128)}, u32[]{:S(2)}, u32[]{:S(2)}) collective-permute-start(f32[576,384]{1,0:T(8,128)S(1)} %fusion.1), channel_id=1, source_target_pairs={{0,1},{1,0},{2,3},{3,2},{4,5},{5,4},{6,7},{7,6},{8,9},{9,8},{10,11... | collective-permute-start | bytes 2654216 | tf_op jit(solution)/shard_map/ppermute | solution.py:116
  73.7 0.5 fusion.3
  74.2 2.0 %collective-permute-done = f32[576,384]{1,0:T(8,128)} collective-permute-done((f32[576,384]{1,0:T(8,128)S(1)}, f32[576,384]{1,0:T(8,128)}, u32[]{:S(2)}, u32[]{:S(2)}) %collective-permute-start) | collective-permute-done | bytes 884768 | tf_op jit(solution)/shard_map/ppermute | solution.py:116
  76.2 2.2 %add.57 = f32[576,384]{1,0:T(8,128)} add(f32[576,384]{1,0:T(8,128)S(1)} %fusion.3, f32[576,384]{1,0:T(8,128)} %collective-permute-done) | non-fusion elementwise | flops 221184 | bytes 2654208 | tf_op jit(solution)/shard_map/add | solution.py:118
  78.4 0.0 copy-start
  78.4 0.0 copy-start.1
  78.4 10.8 %all-to-all-start.1 = ((f32[8,72,384]{2,1,0:T(8,128)}), f32[8,72,384]{2,1,0:T(8,128)S(1)}, u32[]{:S(2)}, u32[]{:S(2)}) async-start(f32[8,72,384]{2,1,0:T(8,128)} %bitcast.2), calls=%async_computation.1 | async-start | bytes 1769472 | tf_op jit(solution)/shard_map/all_to_all | solution.py:22
  89.2 0.0 copy-done
  89.2 0.6 dynamic_slice.20
  89.8 0.0 copy-done.1
  89.8 0.6 gather_fusion
  90.5 0.8 dynamic_slice.21
  91.2 0.6 broadcast_add_fusion
  91.9 0.1 broadcast_subtract_fusion
  91.9 0.1 sub.41
  92.0 0.8 dynamic_slice.23
  92.8 0.1 dynamic_slice.22
  92.9 9.1 %all-to-all-done.1 = f32[8,72,384]{2,1,0:T(8,128)S(1)} async-done(((f32[8,72,384]{2,1,0:T(8,128)}), f32[8,72,384]{2,1,0:T(8,128)S(1)}, u32[]{:S(2)}, u32[]{:S(2)}) %all-to-all-start.1) | async-done | bytes 884768 | tf_op jit(solution)/shard_map/all_to_all | solution.py:22
  102.0 0.1 divide_convert_fusion
  102.1 0.1 broadcast_in_dim.5
  102.2 16.5 %all_to_all.20 = bf16[16,72,384]{2,1,0:T(8,128)(2,1)S(1)} all-to-all(bf16[16,72,384]{2,1,0:T(8,128)(2,1)S(1)} %broadcast_in_dim.5), channel_id=1, replica_groups=mesh['y1'=2,'y0'=2,'z2'=2,'z1'=2,'z0'=2,'y2'=2,'x2'=2,'x1'=2,'x0'=2,'c'=..., dimensions={0} | all-to-all | bytes 1769472 | tf_op jit(solution)/shard_map/all_to_all | solution.py:22
  118.7 0.8 fusion
  119.5 37.2 %all_to_all.21.in_ref = bf16[64,8,576]{2,1,0:T(8,128)(2,1)} all-to-all(bf16[64,8,576]{2,1,0:T(8,128)(2,1)S(1)} %fusion), channel_id=1, replica_groups=mesh['y1'=2,'y0'=2,'z2'=2,'z1'=2,'z0'=2,'y2'=2,'x2'=2,'x1'=2,'x0'=2,'c'=..., dimensions={0} | all-to-all | bytes 1179648 | tf_op jit(solution)/shard_map/all_to_all | solution.py:22
  156.7 2.4 %shard_map.56 = f32[10,8,3072]{2,1,0:T(8,128)} custom-call(s32[3]{0:T(128)} %left_ref.3, bf16[64,8,576]{2,1,0:T(8,128)(2,1)} %all_to_all.21.in_ref), custom_call_target="tpu_custom_call" | custom-call | tf_op jit(solution)/shard_map/pallas_call | solution.py:82
  (3 shorter events, 0.1 us)
Async XLA Ops:
  3.6 67.6 %all-to-all-start = ((bf16[64,8,1344]{2,1,0:T(8,128)(2,1)}), bf16[64,8,1344]{2,1,0:T(8,128)(2,1)S(1)}, u32[]{:S(2)}, u32[]{:S(2)}) async-start(bf16[64,8,1344]{2,1,0:T(8,128)(2,1)} %shard_map.55), calls=%async_computation | async-start | bytes 2883584 | tf_op jit(solution)/shard_map/all_to_all | solution.py:22
  71.8 4.5 %collective-permute-start = (f32[576,384]{1,0:T(8,128)S(1)}, f32[576,384]{1,0:T(8,128)}, u32[]{:S(2)}, u32[]{:S(2)}) collective-permute-start(f32[576,384]{1,0:T(8,128)S(1)} %fusion.1), channel_id=1, source_target_pairs={{0,1},{1,0},{2,3},{3,2},{4,5},{5,4},{6,7},{7,6},{8,9},{9,8},{10,11... | collective-permute-start | bytes 2654216 | tf_op jit(solution)/shard_map/ppermute | solution.py:116
  78.4 10.8 %copy-start = (f32[10]{0:T(128)S(1)}, f32[10]{0:T(128)}, u32[]{:S(2)}) copy-start(f32[10]{0:T(128)} %param.6) | copy-start | bytes 124
  78.4 11.4 %copy-start.1 = (s32[3]{0:T(128)S(1)}, s32[3]{0:T(128)}, u32[]{:S(2)}) copy-start(s32[3]{0:T(128)} %left_ref.3) | copy-start | bytes 40
  78.4 23.6 %all-to-all-start.1 = ((f32[8,72,384]{2,1,0:T(8,128)}), f32[8,72,384]{2,1,0:T(8,128)S(1)}, u32[]{:S(2)}, u32[]{:S(2)}) async-start(f32[8,72,384]{2,1,0:T(8,128)} %bitcast.2), calls=%async_computation.1 | async-start | bytes 1769472 | tf_op jit(solution)/shard_map/all_to_all | solution.py:22

commit v3 on v2

--- a/solution.py
+++ b/solution.py
@@ -14,7 +14,6 @@
 AB_BITS = A_BITS + B_BITS
 B_SUM_BITS = ("c",)
 A_SUM_BITS = ("x0", "y0", "z0")
-SUM_BITS = B_SUM_BITS + A_SUM_BITS
 INTERPRET = False
 
 
@@ -97,27 +96,14 @@
     a_width, b_width = virtuals // a_parts, virtuals // b_parts
     pa_width = pairs * a_width
     sub_rows, sub_cols = pa_width // a_subs, b_width // b_subs
-    peers, subs = a_parts * b_parts, a_subs * b_subs
+    peers = a_parts * b_parts
     group_rows = peers * rows
 
     second_occ = right_occ[0]
     packed = pack_rows(left_list, right_occ, b_tensor, a_parts, b_parts)
     got = exchange(packed, AB_BITS)
-    got = got.reshape(group_rows, b_width + pa_width)
-    right = got[:, :b_width]
-    left = got[:, b_width:]
 
     b_sub = lax.axis_index(B_SUM_BITS)
-
-    def partial_of(half):
-        cols = lax.dynamic_slice_in_dim(right, half * sub_cols, sub_cols, axis=1)
-        return lax.dot_general(left, cols, (((0,), (0,)), ((), ())), preferred_element_type=jnp.float32)
-
-    received = lax.ppermute(partial_of(1 - b_sub), B_SUM_BITS, [(0, 1), (1, 0)])
-    own = lax.optimization_barrier(partial_of(b_sub))
-    paired = own + received
-    shares = exchange(paired.reshape(a_subs, sub_rows, sub_cols), A_SUM_BITS).sum(axis=0)
-
     a_rank, b_rank = lax.axis_index(A_BITS), lax.axis_index(B_BITS)
     a_sub = lax.axis_index(A_SUM_BITS)
     vir_a = lax.dynamic_slice_in_dim(vir_energy, a_rank * a_width, a_width)
@@ -125,13 +111,38 @@
     row_part = (shift[:, None] - vir_a[None, :]).reshape(pa_width)
     row_part = lax.dynamic_slice_in_dim(row_part, a_sub * sub_rows, sub_rows)
     vir_b = lax.dynamic_slice_in_dim(vir_energy, b_rank * b_width + b_sub * sub_cols, sub_cols)
+    got, row_part, vir_b = lax.optimization_barrier((got, row_part, vir_b))
+
+    got = got.reshape(group_rows, b_width + pa_width)
+    right = got[:, :b_width]
+    left = got[:, b_width:]
+
+    def half_of(half):
+        return lax.dynamic_slice_in_dim(right, half * sub_cols, sub_cols, axis=1)
+
+    swap = [(0, 1), (1, 0)]
+
+    def partial_of(half):
+        cols = half_of(half)
+        return lax.dot_general(left, cols, (((0,), (0,)), ((), ())), preferred_element_type=jnp.float32)
+
+    received = lax.ppermute(partial_of(1 - b_sub), B_SUM_BITS, swap)
+    own = lax.optimization_barrier(partial_of(b_sub))
+    paired = own + received
+    shares = exchange(paired.reshape(a_subs, sub_rows, sub_cols), A_SUM_BITS).sum(axis=0)
+
     denominator = row_part[:, None] - vir_b[None, :]
     amp_tile = (shares / denominator).astype(jnp.bfloat16)
 
-    amps = exchange(jnp.broadcast_to(amp_tile[None], (subs, sub_rows, sub_cols)), SUM_BITS)
-    amps = amps.reshape(b_subs, pa_width, sub_cols)
-    halves = right.reshape(group_rows, b_subs, sub_cols)
-    contrib = lax.dot_general(halves, amps, (((1, 2), (0, 2)), ((), ())), preferred_element_type=jnp.float32)
+    amps = exchange(jnp.broadcast_to(amp_tile[None], (a_subs, sub_rows, sub_cols)), A_SUM_BITS)
+    amps = amps.reshape(pa_width, sub_cols)
+    other_amps = lax.ppermute(amps, B_SUM_BITS, swap)
+
+    def contribution(cols, amp_cols):
+        return lax.dot_general(cols, amp_cols, (((1,), (1,)), ((), ())), preferred_element_type=jnp.float32)
+
+    own = lax.optimization_barrier(contribution(half_of(b_sub), amps))
+    contrib = own + contribution(half_of(1 - b_sub), other_amps)
     returned = exchange(contrib.reshape(peers, rows, pa_width).astype(jnp.bfloat16), AB_BITS)
     return place_rows(left_list, returned, occ_count, a_parts, b_parts)
 

time: 160 us -> 156 us (0.975)
  the two profiles are of different devices: /device:TPU:2 before, /device:TPU:1 now
where the time goes in v3:
time: 156 us; the launch traced here: 155 us
  blocking collectives  60.1 us (39%)
  waiting for transfers between devices  45.2 us (29%)
  starting transfers between devices  36.2 us (23%)
  Pallas kernels  5.29 us (3%)
  local copies, waits for them, and re-layouts  3.33 us (2%)
  other arithmetic  2.2 us (1%)
  matrix products  2 us (1%)
    all_to_all x3, blocking collectives, exchange(): return lax.all_to_all(x, axes, split_axis=0, concat_axis=0, tiled=True)  60.1 us
    all_to_all x1, waiting for transfers between devices, exchange(): return lax.all_to_all(x, axes, split_axis=0, concat_axis=0, tiled=True)  42.6 us
    all_to_all x1, starting transfers between devices, exchange(): return lax.all_to_all(x, axes, split_axis=0, concat_axis=0, tiled=True)  28 us
    ppermute x1, starting transfers between devices, body(): other_amps = lax.ppermute(amps, B_SUM_BITS, swap)  4.86 us
    ppermute x1, starting transfers between devices, body(): received = lax.ppermute(partial_of(1 - b_sub), B_SUM_BITS, swap)  3.39 us
  transfers between devices with their start and end apart: 3, of which 3 were waited for; matrix products, arithmetic and copies ran while one was open for 3% of the time, Pallas kernels for 0%

profile of v3, /device:TPU:1, one launch (start us, length us, event | category | flops | bytes accessed | tf_op | source)
XLA Modules:
  0.0 155.1 jit_solution(4726531663499984333)
XLA Ops:
  0.7 2.9 %shard_map.55 = bf16[64,8,1344]{2,1,0:T(8,128)(2,1)} custom-call(s32[3]{0:T(128)} %left_ref.3, s32[1]{0:T(128)} %copy.8.right_ref, bf16[10,8,3072]{2,1,0:T(8,128)(2,1)} %b_ref.1), custom_call_target="tpu_custom_call" | custom-call | tf_op jit(solution)/shard_map/pallas_call | solution.py:48
  3.6 0.0 copy-start
  3.6 0.0 copy-start.1
  3.6 28.0 %all-to-all-start = ((bf16[64,8,1344]{2,1,0:T(8,128)(2,1)}), bf16[64,8,1344]{2,1,0:T(8,128)(2,1)S(1)}, u32[]{:S(2)}, u32[]{:S(2)}) async-start(bf16[64,8,1344]{2,1,0:T(8,128)(2,1)} %shard_map.55), calls=%async_computation | async-start | bytes 2883584 | tf_op jit(solution)/shard_map/all_to_all | solution.py:21
  31.6 0.8 dynamic_slice.21
  32.4 0.8 dynamic_slice.23
  33.2 0.0 copy-done
  33.2 0.6 dynamic_slice.20
  33.8 0.0 copy-done.1
  33.8 0.6 gather_fusion
  34.4 0.6 broadcast_add_fusion
  35.1 0.1 broadcast_subtract_fusion
  35.1 0.1 sub.41
  35.2 0.1 dynamic_slice.22
  35.3 42.6 %all-to-all-done = bf16[64,8,1344]{2,1,0:T(8,128)(2,1)S(1)} async-done(((bf16[64,8,1344]{2,1,0:T(8,128)(2,1)}), bf16[64,8,1344]{2,1,0:T(8,128)(2,1)S(1)}, u32[]{:S(2)}, u32[]{:S(2)}) %all-to-all-start) | async-done | bytes 1376288 | tf_op jit(solution)/shard_map/all_to_all | solution.py:21
  77.9 0.1 slice.10
  78.0 0.5 fusion.1
  78.5 3.4 %collective-permute-start = (f32[576,384]{1,0:T(8,128)S(1)}, f32[576,384]{1,0:T(8,128)}, u32[]{:S(2)}, u32[]{:S(2)}) collective-permute-start(f32[576,384]{1,0:T(8,128)S(1)} %fusion.1), channel_id=1, source_target_pairs={{0,1},{1,0},{2,3},{3,2},{4,5},{5,4},{6,7},{7,6},{8,9},{9,8},{10,11... | collective-permute-start | bytes 2654216 | tf_op jit(solution)/shard_map/ppermute | solution.py:129
  81.9 0.5 fusion.3
  82.4 1.7 %collective-permute-done = f32[576,384]{1,0:T(8,128)} collective-permute-done((f32[576,384]{1,0:T(8,128)S(1)}, f32[576,384]{1,0:T(8,128)}, u32[]{:S(2)}, u32[]{:S(2)}) %collective-permute-start) | collective-permute-done | bytes 884768 | tf_op jit(solution)/shard_map/ppermute | solution.py:129
  84.1 1.3 add.76
  85.4 15.4 %all_to_all.20 = f32[8,72,384]{2,1,0:T(8,128)S(1)} all-to-all(f32[8,72,384]{2,1,0:T(8,128)S(1)} %bitcast.14), channel_id=1, replica_groups=mesh['y1'=2,'y0'=2,'z2'=2,'z1'=2,'z0'=2,'y2'=2,'x2'=2,'x1'=2,'x0'=2,'c'=..., dimensions={0} | all-to-all | bytes 1769472 | tf_op jit(solution)/shard_map/all_to_all | solution.py:21
  100.9 0.1 divide_convert_fusion
  101.0 9.1 %all_to_all.21 = bf16[8,72,384]{2,1,0:T(8,128)(2,1)S(1)} all-to-all(bf16[8,72,384]{2,1,0:T(8,128)(2,1)S(1)} %broadcast_in_dim.5), channel_id=1, replica_groups=mesh['y1'=2,'y0'=2,'z2'=2,'z1'=2,'z0'=2,'y2'=2,'x2'=2,'x1'=2,'x0'=2,'c'=..., dimensions={0} | all-to-all | bytes 884736 | tf_op jit(solution)/shard_map/all_to_all | solution.py:21
  110.1 4.9 %collective-permute-start.1 = (bf16[576,384]{1,0:T(8,128)(2,1)S(1)}, bf16[576,384]{1,0:T(8,128)(2,1)S(1)}, u32[]{:S(2)}, u32[]{:S(2)}) collective-permute-start(bf16[576,384]{1,0:T(8,128)(2,1)S(1)} %bitcast.16), channel_id=1, source_target_pairs={{0,1},{1,0},{2,3},{3,2},{4,5},{5,4},{6,7},{7,6},{8,9},{9,8},{10,11... | collective-permute-start | bytes 1327112 | tf_op jit(solution)/shard_map/ppermute | solution.py:139
  114.9 0.5 fusion.7
  115.5 0.9 collective-permute-done.1
  116.3 0.5 fusion
  116.9 0.3 copy.7
  117.2 35.6 %all_to_all.22.in_ref = bf16[64,8,576]{2,1,0:T(8,128)(2,1)} all-to-all(bf16[64,8,576]{2,1,0:T(8,128)(2,1)S(1)} %bitcast.15), channel_id=1, replica_groups=mesh['y1'=2,'y0'=2,'z2'=2,'z1'=2,'z0'=2,'y2'=2,'x2'=2,'x1'=2,'x0'=2,'c'=..., dimensions={0} | all-to-all | bytes 1179648 | tf_op jit(solution)/shard_map/all_to_all | solution.py:21
  152.7 2.4 %shard_map.56 = f32[10,8,3072]{2,1,0:T(8,128)} custom-call(s32[3]{0:T(128)} %left_ref.3, bf16[64,8,576]{2,1,0:T(8,128)(2,1)} %all_to_all.22.in_ref), custom_call_target="tpu_custom_call" | custom-call | tf_op jit(solution)/shard_map/pallas_call | solution.py:81
  (4 shorter events, 0.1 us)
Async XLA Ops:
  3.6 29.6 %copy-start = (f32[10]{0:T(128)S(1)}, f32[10]{0:T(128)}, u32[]{:S(2)}) copy-start(f32[10]{0:T(128)} %param.6) | copy-start | bytes 124
  3.6 30.2 %copy-start.1 = (s32[3]{0:T(128)S(1)}, s32[3]{0:T(128)}, u32[]{:S(2)}) copy-start(s32[3]{0:T(128)} %left_ref.3) | copy-start | bytes 40
  3.6 74.3 %all-to-all-start = ((bf16[64,8,1344]{2,1,0:T(8,128)(2,1)}), bf16[64,8,1344]{2,1,0:T(8,128)(2,1)S(1)}, u32[]{:S(2)}, u32[]{:S(2)}) async-start(bf16[64,8,1344]{2,1,0:T(8,128)(2,1)} %shard_map.55), calls=%async_computation | async-start | bytes 2883584 | tf_op jit(solution)/shard_map/all_to_all | solution.py:21
  78.5 5.6 %collective-permute-start = (f32[576,384]{1,0:T(8,128)S(1)}, f32[576,384]{1,0:T(8,128)}, u32[]{:S(2)}, u32[]{:S(2)}) collective-permute-start(f32[576,384]{1,0:T(8,128)S(1)} %fusion.1), channel_id=1, source_target_pairs={{0,1},{1,0},{2,3},{3,2},{4,5},{5,4},{6,7},{7,6},{8,9},{9,8},{10,11... | collective-permute-start | bytes 2654216 | tf_op jit(solution)/shard_map/ppermute | solution.py:129
  110.1 6.3 %collective-permute-start.1 = (bf16[576,384]{1,0:T(8,128)(2,1)S(1)}, bf16[576,384]{1,0:T(8,128)(2,1)S(1)}, u32[]{:S(2)}, u32[]{:S(2)}) collective-permute-start(bf16[576,384]{1,0:T(8,128)(2,1)S(1)} %bitcast.16), channel_id=1, source_target_pairs={{0,1},{1,0},{2,3},{3,2},{4,5},{5,4},{6,7},{7,6},{8,9},{9,8},{10,11... | collective-permute-start | bytes 1327112 | tf_op jit(solution)/shard_map/ppermute | solution.py:139

commit v4 on v3

v4 whole, which is shorter than its diff:
```python
import jax
import jax.numpy as jnp
import numpy as np
from jax import lax
from jax.experimental import pallas as pl
from jax.experimental.pallas import tpu as pltpu
from jax.sharding import Mesh, PartitionSpec as P

GRP_BITS = ("y1", "y0", "z2", "z1", "z0")
INNER_BITS = ("y2", "x2", "x1", "x0", "c")
ALL_BITS = GRP_BITS + INNER_BITS
A_BITS = ("x2", "x1", "y2", "y1")
B_BITS = ("z2", "z1")
B_SUM_BITS = ("c",)
A_SUM_BITS = ("x0", "y0", "z0")
INTERPRET = False


def exchange(x, axes):
    return lax.all_to_all(x, axes, split_axis=0, concat_axis=0, tiled=True)


def pick_columns(orbitals, b_tensor, parts, lanes):
    _, rows, virtuals = b_tensor.shape
    count = orbitals.shape[0]
    width = virtuals // parts

    def kernel(orbital_ref, b_ref, out_ref, buf, sems):
        copies = []
        for k in range(count):
            copies.append(pltpu.make_async_copy(b_ref.at[orbital_ref[k]], buf.at[k], sems.at[k]))
            copies[-1].start()
        for k in range(count):
            copies[k].wait()
            for part in range(parts):
                out_ref[part, :, k * width : (k + 1) * width] = buf[k, :, part * width : (part + 1) * width]
        if count * width < lanes:
            out_ref[:, :, count * width :] = jnp.zeros((parts, rows, lanes - count * width), out_ref.dtype)

    return pl.pallas_call(
        kernel,
        out_shape=jax.ShapeDtypeStruct((parts, rows, lanes), b_tensor.dtype),
        in_specs=[pl.BlockSpec(memory_space=pltpu.SMEM), pl.BlockSpec(memory_space=pl.ANY)],
        out_specs=pl.BlockSpec(memory_space=pltpu.VMEM),
        scratch_shapes=[pltpu.VMEM((count, rows, virtuals), b_tensor.dtype), pltpu.SemaphoreType.DMA((count,))],
        interpret=INTERPRET,
    )(orbitals, b_tensor)


def place_rows(left_list, returned, occ_count):
    a_parts, rows, pa_width = returned.shape
    pairs = left_list.shape[0]
    a_width = pa_width // pairs
    virtuals = a_parts * a_width

    def kernel(left_ref, in_ref, out_ref, rows_ref):
        for a in range(a_parts):
            for p in range(pairs):
                rows_ref[p, :, a * a_width : (a + 1) * a_width] = in_ref[a, :, p * a_width : (p + 1) * a_width]
        for orbital in range(occ_count):
            total = jnp.zeros((rows, virtuals), jnp.float32)
            for p in range(pairs):
                total = total + jnp.where(left_ref[p] == orbital, rows_ref[p], 0.0)
            out_ref[orbital] = total

    return pl.pallas_call(
        kernel,
        out_shape=jax.ShapeDtypeStruct((occ_count, rows, virtuals), jnp.float32),
        in_specs=[pl.BlockSpec(memory_space=pltpu.SMEM), pl.BlockSpec(memory_space=pltpu.VMEM)],
        out_specs=pl.BlockSpec(memory_space=pltpu.VMEM),
        scratch_shapes=[pltpu.VMEM((pairs, rows, virtuals), jnp.float32)],
        interpret=INTERPRET,
    )(left_list, returned)


def body(b_tensor, occ_energy, vir_energy, left_list, right_occ):
    occ_count, rows, virtuals = b_tensor.shape
    pairs = left_list.shape[0]
    a_parts, b_parts = 2 ** len(A_BITS), 2 ** len(B_BITS)
    a_subs, b_subs = 2 ** len(A_SUM_BITS), 2 ** len(B_SUM_BITS)
    a_width, b_width = virtuals // a_parts, virtuals // b_parts
    pa_width = pairs * a_width
    sub_rows, sub_cols = pa_width // a_subs, b_width // b_subs
    group_rows = a_parts * b_parts * rows

    second_occ = right_occ[0]
    right = exchange(pick_columns(right_occ, b_tensor, b_parts, b_width), B_BITS)

    b_sub = lax.axis_index(B_SUM_BITS)
    a_rank, b_rank = lax.axis_index(A_BITS), lax.axis_index(B_BITS)
    a_sub = lax.axis_index(A_SUM_BITS)
    vir_a = lax.dynamic_slice_in_dim(vir_energy, a_rank * a_width, a_width)
    shift = occ_energy[left_list] + occ_energy[second_occ]
    row_part = (shift[:, None] - vir_a[None, :]).reshape(pa_width)
    row_part = lax.dynamic_slice_in_dim(row_part, a_sub * sub_rows, sub_rows)
    vir_b = lax.dynamic_slice_in_dim(vir_energy, b_rank * b_width + b_sub * sub_cols, sub_cols)
    left = pick_columns(left_list, b_tensor, a_parts, b_width)
    right, left, row_part, vir_b = lax.optimization_barrier((right, left, row_part, vir_b))

    right = jnp.broadcast_to(right.reshape(1, b_parts * rows, b_width), (a_parts, b_parts * rows, b_width))
    got = exchange(jnp.concatenate([right, left], axis=1), A_BITS)
    right = got[:, : b_parts * rows].reshape(a_parts, b_parts, rows, b_width)
    right = right.transpose(1, 0, 2, 3).reshape(group_rows, b_width)
    left = got[:, b_parts * rows :, :pa_width].reshape(1, a_parts * rows, pa_width)
    left = exchange(jnp.broadcast_to(left, (b_parts, a_parts * rows, pa_width)), B_BITS)
    left = left.reshape(group_rows, pa_width)

    def half_of(half):
        return lax.dynamic_slice_in_dim(right, half * sub_cols, sub_cols, axis=1)

    swap = [(0, 1), (1, 0)]

    def partial_of(half):
        cols = half_of(half)
        return lax.dot_general(left, cols, (((0,), (0,)), ((), ())), preferred_element_type=jnp.float32)

    received = lax.ppermute(partial_of(1 - b_sub), B_SUM_BITS, swap)
    own = lax.optimization_barrier(partial_of(b_sub))
    paired = own + received
    shares = exchange(paired.reshape(a_subs, sub_rows, sub_cols), A_SUM_BITS).sum(axis=0)

    denominator = row_part[:, None] - vir_b[None, :]
    amp_tile = (shares / denominator).astype(jnp.bfloat16)

    amps = exchange(jnp.broadcast_to(amp_tile[None], (a_subs, sub_rows, sub_cols)), A_SUM_BITS)
    amps = amps.reshape(pa_width, sub_cols)
    other_amps = lax.ppermute(amps, B_SUM_BITS, swap)

    def contribution(cols, amp_cols):
        return lax.dot_general(cols, amp_cols, (((1,), (1,)), ((), ())), preferred_element_type=jnp.float32)

    own = lax.optimization_barrier(contribution(half_of(b_sub), amps))
    contrib = own + contribution(half_of(1 - b_sub), other_amps)
    parts = exchange(contrib.astype(jnp.bfloat16).reshape(b_parts, a_parts * rows, pa_width), B_BITS)
    returned = exchange(parts.astype(jnp.float32).sum(axis=0).reshape(a_parts, rows, pa_width), A_BITS)
    return place_rows(left_list, returned, occ_count)


def solution(mesh):
    fine = Mesh(np.asarray(mesh.devices).reshape((2,) * len(ALL_BITS)), ALL_BITS)
    placed = (P(None, ALL_BITS, None), P(), P(), P(), P())
    return jax.shard_map(body, mesh=fine, in_specs=placed, out_specs=P(None, ALL_BITS, None), check_vma=False)
```

time: 156 us -> 178 us (1.14); the launches traced: 155 us -> 175 us
  blocking collectives: 60.1 us -> 109 us
  waiting for transfers between devices: 45.2 us -> 12.2 us
  local copies, waits for them, and re-layouts: 3.33 us -> 5.78 us
    all_to_all x3 -> x5, blocking collectives: 60.1 us -> 109 us  [exchange(): return lax.all_to_all(x, axes, split_axis=0, concat_axis=0, tiled=True)]
    all_to_all x1 -> x2, waiting for transfers between devices: 42.6 us -> 9.75 us  [exchange(): return lax.all_to_all(x, axes, split_axis=0, concat_axis=0, tiled=True)]
    ppermute x1, starting transfers between devices: 3.39 us -> 9.11 us  [body(): received = lax.ppermute(partial_of(1 - b_sub), B_SUM_BITS, swap)]
    all_to_all x1 -> x2, starting transfers between devices: 28 us -> 22.9 us  [exchange(): return lax.all_to_all(x, axes, split_axis=0, concat_axis=0, tiled=True)]
    pallas_call x1 -> x2, Pallas kernels: 2.93 us -> 3.83 us  [pick_columns(): pl.pallas_call(kernel, out_shape=jax.ShapeDtypeStruct((parts, rows, lanes...]
  transfers between devices with their start and end apart: 3 -> 4, of which waited for: 3 -> 3; matrix products, arithmetic and copies ran while one was open for 3% -> 4% of each run, Pallas kernels for 0% -> 1%
where the time goes in v4:
time: 178 us; the launch traced here: 175 us
  blocking collectives  109 us (61%)
  starting transfers between devices  36.9 us (21%)
  waiting for transfers between devices  12.2 us (7%)
  Pallas kernels  6.02 us (3%)
  local copies, waits for them, and re-layouts  5.78 us (3%)
  other arithmetic  2.68 us (2%)
  matrix products  1.96 us (1%)
    all_to_all x5, blocking collectives, exchange(): return lax.all_to_all(x, axes, split_axis=0, concat_axis=0, tiled=True)  109 us
    all_to_all x2, starting transfers between devices, exchange(): return lax.all_to_all(x, axes, split_axis=0, concat_axis=0, tiled=True)  22.9 us
    all_to_all x2, waiting for transfers between devices, exchange(): return lax.all_to_all(x, axes, split_axis=0, concat_axis=0, tiled=True)  9.75 us
    ppermute x1, starting transfers between devices, body(): received = lax.ppermute(partial_of(1 - b_sub), B_SUM_BITS, swap)  9.11 us
    ppermute x1, starting transfers between devices, body(): other_amps = lax.ppermute(amps, B_SUM_BITS, swap)  4.86 us
    pallas_call x2, Pallas kernels, pick_columns(): pl.pallas_call(kernel, out_shape=jax.ShapeDtypeStruct((parts, rows, lanes...  3.83 us
  transfers between devices with their start and end apart: 4, of which 3 were waited for; matrix products, arithmetic and copies ran while one was open for 4% of the time, Pallas kernels for 1%

profile of v4, /device:TPU:1, one launch (start us, length us, event | category | flops | bytes accessed | tf_op | source)
XLA Modules:
  0.0 174.9 jit_solution(13331533214156434916)
XLA Ops:
  0.7 1.4 shard_map.55
  2.1 16.3 %all-to-all-start = ((bf16[4,8,768]{2,1,0:T(8,128)(2,1)}), bf16[4,8,768]{2,1,0:T(8,128)(2,1)S(1)}, u32[]{:S(2)}, u32[]{:S(2)}) async-start(bf16[4,8,768]{2,1,0:T(8,128)(2,1)} %shard_map.55), calls=%async_computation | async-start | bytes 98304 | tf_op jit(solution)/shard_map/all_to_all | solution.py:20
  18.4 0.7 compare_select_fusion
  19.1 1.2 dynamic_slice.20
  20.3 1.3 gather_fusion
  21.6 0.8 dynamic_slice.21
  22.4 0.6 broadcast_add_fusion
  23.0 0.1 broadcast_subtract_fusion
  23.1 2.4 %shard_map.56 = bf16[16,8,768]{2,1,0:T(8,128)(2,1)} custom-call(s32[3]{0:T(128)} %left_ref.1, bf16[10,8,3072]{2,1,0:T(8,128)(2,1)} %b_ref.3), custom_call_target="tpu_custom_call" | custom-call | tf_op jit(solution)/shard_map/pallas_call | solution.py:40
  25.5 0.1 sub.41
  25.6 0.8 dynamic_slice.23
  26.4 0.1 dynamic_slice.22
  26.4 0.0 all-to-all-done
  26.4 0.1 broadcast_in_dim.14
  26.5 1.0 pad_maximum_fusion
  27.5 45.5 %all_to_all.35 = bf16[16,40,768]{2,1,0:T(8,128)(2,1)S(1)} all-to-all(bf16[16,40,768]{2,1,0:T(8,128)(2,1)S(1)} %pad_maximum_fusion), channel_id=1, replica_groups=mesh['y1'=2,'y0'=2,'z2'=2,'z1'=2,'z0'=2,'y2'=2,'x2'=2,'x1'=2,'x0'=2,'c'=..., dimensions={0} | all-to-all | bytes 1966080 | tf_op jit(solution)/shard_map/all_to_all | solution.py:20
  73.1 0.1 copy.13
  73.2 0.9 broadcast_in_dim.31
  74.1 6.6 %all-to-all-start.2 = ((bf16[4,128,576]{1,2,0:T(8,128)(2,1)}), bf16[4,128,576]{1,2,0:T(8,128)(2,1)S(1)}, u32[]{:S(2)}, u32[]{:S(2)}) async-start(bf16[4,128,576]{1,2,0:T(8,128)(2,1)} %broadcast_in_dim.31), calls=%async_computation.2 | async-start | bytes 1179648 | tf_op jit(solution)/shard_map/all_to_all | solution.py:20
  80.7 0.1 slice_bitcast_fusion
  80.8 0.1 copy.12
  80.9 9.8 %all-to-all-done.2 = bf16[4,128,576]{1,2,0:T(8,128)(2,1)S(1)} async-done(((bf16[4,128,576]{1,2,0:T(8,128)(2,1)}), bf16[4,128,576]{1,2,0:T(8,128)(2,1)S(1)}, u32[]{:S(2)}, u32[]{:S(2)}) %all-to-all-start.2) | async-done | bytes 589856 | tf_op jit(solution)/shard_map/all_to_all | solution.py:20
  90.6 0.5 fusion.2
  91.1 9.1 %collective-permute-start = (f32[576,384]{1,0:T(8,128)S(1)}, f32[576,384]{1,0:T(8,128)S(1)}, u32[]{:S(2)}, u32[]{:S(2)}) collective-permute-start(f32[576,384]{1,0:T(8,128)S(1)} %fusion.2), channel_id=1, source_target_pairs={{0,1},{1,0},{2,3},{3,2},{4,5},{5,4},{6,7},{7,6},{8,9},{9,8},{10,11... | collective-permute-start | bytes 2654216 | tf_op jit(solution)/shard_map/ppermute | solution.py:117
  100.2 0.5 fusion.4
  100.7 1.5 collective-permute-done
  102.3 0.1 add.76
  102.3 16.2 %all_to_all.36 = f32[8,72,384]{2,1,0:T(8,128)S(1)} all-to-all(f32[8,72,384]{2,1,0:T(8,128)S(1)} %bitcast.39), channel_id=1, replica_groups=mesh['y1'=2,'y0'=2,'z2'=2,'z1'=2,'z0'=2,'y2'=2,'x2'=2,'x1'=2,'x0'=2,'c'=..., dimensions={0} | all-to-all | bytes 1769472 | tf_op jit(solution)/shard_map/all_to_all | solution.py:20
  118.6 0.1 divide_convert_fusion
  118.8 9.1 %all_to_all.37 = bf16[8,72,384]{2,1,0:T(8,128)(2,1)S(1)} all-to-all(bf16[8,72,384]{2,1,0:T(8,128)(2,1)S(1)} %broadcast_in_dim.32), channel_id=1, replica_groups=mesh['y1'=2,'y0'=2,'z2'=2,'z1'=2,'z0'=2,'y2'=2,'x2'=2,'x1'=2,'x0'=2,'c'=..., dimensions={0} | all-to-all | bytes 884736 | tf_op jit(solution)/shard_map/all_to_all | solution.py:20
  127.9 4.9 %collective-permute-start.1 = (bf16[576,384]{1,0:T(8,128)(2,1)S(1)}, bf16[576,384]{1,0:T(8,128)(2,1)S(1)}, u32[]{:S(2)}, u32[]{:S(2)}) collective-permute-start(bf16[576,384]{1,0:T(8,128)(2,1)S(1)} %bitcast.41), channel_id=1, source_target_pairs={{0,1},{1,0},{2,3},{3,2},{4,5},{5,4},{6,7},{7,6},{8,9},{9,8},{10,11... | collective-permute-start | bytes 1327112 | tf_op jit(solution)/shard_map/ppermute | solution.py:127
  132.7 0.5 fusion.10
  133.2 0.9 collective-permute-done.1
  134.1 0.5 fusion.1
  134.6 0.1 copy.30
  134.7 20.6 %all_to_all.38 = bf16[4,128,576]{1,2,0:T(8,128)(2,1)S(1)} all-to-all(bf16[4,128,576]{1,2,0:T(8,128)(2,1)S(1)} %bitcast.40), channel_id=1, replica_groups=mesh['y1'=2,'y0'=2,'z2'=2,'z1'=2,'z0'=2,'y2'=2,'x2'=2,'x1'=2,'x0'=2,'c'=..., dimensions={0} | all-to-all | bytes 1179648 | tf_op jit(solution)/shard_map/all_to_all | solution.py:20
  155.4 0.1 convert_reduce_fusion
  155.4 0.2 copy.17
  155.6 17.0 %all_to_all.39.in_ref = f32[16,8,576]{2,1,0:T(8,128)} all-to-all(f32[16,8,576]{2,1,0:T(8,128)S(1)} %bitcast.43), channel_id=1, replica_groups=mesh['y1'=2,'y0'=2,'z2'=2,'z1'=2,'z0'=2,'y2'=2,'x2'=2,'x1'=2,'x0'=2,'c'=..., dimensions={0} | all-to-all | bytes 589824 | tf_op jit(solution)/shard_map/all_to_all | solution.py:20
  172.7 2.2 %shard_map.57 = f32[10,8,3072]{2,1,0:T(8,128)} custom-call(s32[3]{0:T(128)} %left_ref.1, f32[16,8,576]{2,1,0:T(8,128)} %all_to_all.39.in_ref), custom_call_target="tpu_custom_call" | custom-call | tf_op jit(solution)/shard_map/pallas_call | solution.py:66
  (4 shorter events, 0.1 us)
Async XLA Ops:
  2.1 24.3 %all-to-all-start = ((bf16[4,8,768]{2,1,0:T(8,128)(2,1)}), bf16[4,8,768]{2,1,0:T(8,128)(2,1)S(1)}, u32[]{:S(2)}, u32[]{:S(2)}) async-start(bf16[4,8,768]{2,1,0:T(8,128)(2,1)} %shard_map.55), calls=%async_computation | async-start | bytes 98304 | tf_op jit(solution)/shard_map/all_to_all | solution.py:20
  74.1 16.5 %all-to-all-start.2 = ((bf16[4,128,576]{1,2,0:T(8,128)(2,1)}), bf16[4,128,576]{1,2,0:T(8,128)(2,1)S(1)}, u32[]{:S(2)}, u32[]{:S(2)}) async-start(bf16[4,128,576]{1,2,0:T(8,128)(2,1)} %broadcast_in_dim.31), calls=%async_computation.2 | async-start | bytes 1179648 | tf_op jit(solution)/shard_map/all_to_all | solution.py:20
  91.1 11.2 %collective-permute-start = (f32[576,384]{1,0:T(8,128)S(1)}, f32[576,384]{1,0:T(8,128)S(1)}, u32[]{:S(2)}, u32[]{:S(2)}) collective-permute-start(f32[576,384]{1,0:T(8,128)S(1)} %fusion.2), channel_id=1, source_target_pairs={{0,1},{1,0},{2,3},{3,2},{4,5},{5,4},{6,7},{7,6},{8,9},{9,8},{10,11... | collective-permute-start | bytes 2654216 | tf_op jit(solution)/shard_map/ppermute | solution.py:117
  127.9 6.3 %collective-permute-start.1 = (bf16[576,384]{1,0:T(8,128)(2,1)S(1)}, bf16[576,384]{1,0:T(8,128)(2,1)S(1)}, u32[]{:S(2)}, u32[]{:S(2)}) collective-permute-start(bf16[576,384]{1,0:T(8,128)(2,1)S(1)} %bitcast.41), channel_id=1, source_target_pairs={{0,1},{1,0},{2,3},{3,2},{4,5},{5,4},{6,7},{7,6},{8,9},{9,8},{10,11... | collective-permute-start | bytes 1327112 | tf_op jit(solution)/shard_map/ppermute | solution.py:127

commit v5 on v3

--- a/solution.py
+++ b/solution.py
@@ -9,11 +9,11 @@
 GRP_BITS = ("y1", "y0", "z2", "z1", "z0")
 INNER_BITS = ("y2", "x2", "x1", "x0", "c")
 ALL_BITS = GRP_BITS + INNER_BITS
-A_BITS = ("x2", "x1", "y2", "y1")
-B_BITS = ("z2", "z1")
+A_BITS = ("y2", "y1", "y0", "z2")
+B_BITS = ("z1", "z0")
 AB_BITS = A_BITS + B_BITS
 B_SUM_BITS = ("c",)
-A_SUM_BITS = ("x0", "y0", "z0")
+A_SUM_BITS = ("x2", "x1", "x0")
 INTERPRET = False
 
 
@@ -88,6 +88,17 @@
     )(left_list, returned)
 
 
+def sum_over_ring(parts):
+    ring, rows, cols = parts.shape
+    largest = jnp.max(jnp.abs(parts))
+    exponent = jnp.clip(14.0 - jnp.ceil(jnp.log2(jnp.maximum(largest, 1e-37))), -100.0, 100.0)
+    scaled = (parts * jnp.exp2(exponent)).astype(jnp.float16)
+    tag = jnp.full((ring, 8, cols), exponent, jnp.float16)
+    got = exchange(jnp.concatenate([scaled, tag], axis=1), A_SUM_BITS)
+    undo = jnp.exp2(-got[:, rows : rows + 1].astype(jnp.float32))
+    return (got[:, :rows].astype(jnp.float32) * undo).sum(axis=0)
+
+
 def body(b_tensor, occ_energy, vir_energy, left_list, right_occ):
     occ_count, rows, virtuals = b_tensor.shape
     pairs = left_list.shape[0]
@@ -129,7 +140,7 @@
     received = lax.ppermute(partial_of(1 - b_sub), B_SUM_BITS, swap)
     own = lax.optimization_barrier(partial_of(b_sub))
     paired = own + received
-    shares = exchange(paired.reshape(a_subs, sub_rows, sub_cols), A_SUM_BITS).sum(axis=0)
+    shares = sum_over_ring(paired.reshape(a_subs, sub_rows, sub_cols))
 
     denominator = row_part[:, None] - vir_b[None, :]
     amp_tile = (shares / denominator).astype(jnp.bfloat16)

time: 156 us -> 151 us (0.968); the launches traced: 155 us -> 148 us
  waiting for transfers between devices: 45.2 us -> 33.7 us
  blocking collectives: 60.1 us -> 64.2 us
    all_to_all x1, waiting for transfers between devices: 42.6 us -> 31.1 us  [exchange(): return lax.all_to_all(x, axes, split_axis=0, concat_axis=0, tiled=True)]
    all_to_all x3, blocking collectives: 60.1 us -> 64.2 us  [exchange(): return lax.all_to_all(x, axes, split_axis=0, concat_axis=0, tiled=True)]
    all_to_all x1, starting transfers between devices: 28 us -> 24 us  [exchange(): return lax.all_to_all(x, axes, split_axis=0, concat_axis=0, tiled=True)]
    ppermute x1, starting transfers between devices: 3.39 us -> 6.12 us  [body(): received = lax.ppermute(partial_of(1 - b_sub), B_SUM_BITS, swap)]
where the time goes in v5:
time: 151 us; the launch traced here: 148 us
  blocking collectives  64.2 us (43%)
  starting transfers between devices  35.6 us (24%)
  waiting for transfers between devices  33.7 us (22%)
  Pallas kernels  5.29 us (4%)
  local copies, waits for them, and re-layouts  3.43 us (2%)
  matrix products  2.91 us (2%)
  other arithmetic  1.69 us (1%)
  between operations  1.56 us (1%)
    all_to_all x3, blocking collectives, exchange(): return lax.all_to_all(x, axes, split_axis=0, concat_axis=0, tiled=True)  64.2 us
    all_to_all x1, waiting for transfers between devices, exchange(): return lax.all_to_all(x, axes, split_axis=0, concat_axis=0, tiled=True)  31.1 us
    all_to_all x1, starting transfers between devices, exchange(): return lax.all_to_all(x, axes, split_axis=0, concat_axis=0, tiled=True)  24 us
    ppermute x1, starting transfers between devices, body(): received = lax.ppermute(partial_of(1 - b_sub), B_SUM_BITS, swap)  6.12 us
    ppermute x1, starting transfers between devices, body(): other_amps = lax.ppermute(amps, B_SUM_BITS, swap)  5.46 us
  transfers between devices with their start and end apart: 3, of which 3 were waited for; matrix products, arithmetic and copies ran while one was open for 3% of the time, Pallas kernels for 0%

profile of v5, /device:TPU:1, one launch (start us, length us, event | category | flops | bytes accessed | tf_op | source)
XLA Modules:
  0.0 148.3 jit_solution(5002861945084442677)
XLA Ops:
  0.7 2.9 %shard_map.55 = bf16[64,8,1344]{2,1,0:T(8,128)(2,1)} custom-call(s32[3]{0:T(128)} %left_ref.3, s32[1]{0:T(128)} %copy.15.right_ref, bf16[10,8,3072]{2,1,0:T(8,128)(2,1)} %b_ref.1), custom_call_target="tpu_custom_call" | custom-call | tf_op jit(solution)/shard_map/pallas_call | solution.py:48
  3.6 0.0 copy-start
  3.6 0.0 copy-start.1
  3.6 24.0 %all-to-all-start = ((bf16[64,8,1344]{2,1,0:T(8,128)(2,1)}), bf16[64,8,1344]{2,1,0:T(8,128)(2,1)S(1)}, u32[]{:S(2)}, u32[]{:S(2)}) async-start(bf16[64,8,1344]{2,1,0:T(8,128)(2,1)} %shard_map.55), calls=%async_computation | async-start | bytes 2883584 | tf_op jit(solution)/shard_map/all_to_all | solution.py:21
  27.6 0.8 dynamic_slice.21
  28.4 0.8 dynamic_slice.23
  29.2 0.0 copy-done
  29.2 0.6 dynamic_slice.20
  29.7 0.0 copy-done.1
  29.8 0.6 gather_fusion
  30.4 0.6 broadcast_add_fusion
  31.1 0.1 broadcast_subtract_fusion
  31.1 0.1 sub.44
  31.2 0.1 dynamic_slice.22
  31.3 31.1 %all-to-all-done = bf16[64,8,1344]{2,1,0:T(8,128)(2,1)S(1)} async-done(((bf16[64,8,1344]{2,1,0:T(8,128)(2,1)}), bf16[64,8,1344]{2,1,0:T(8,128)(2,1)S(1)}, u32[]{:S(2)}, u32[]{:S(2)}) %all-to-all-start) | async-done | bytes 1376288 | tf_op jit(solution)/shard_map/all_to_all | solution.py:21
  62.4 0.1 slice.18
  62.4 1.4 fusion.1
  63.8 6.1 %collective-permute-start = (f32[576,384]{1,0:T(8,128)}, f32[576,384]{1,0:T(8,128)S(1)}, u32[]{:S(2)}, u32[]{:S(2)}) collective-permute-start(f32[576,384]{1,0:T(8,128)} %fusion.1), channel_id=1, source_target_pairs={{0,1},{1,0},{2,3},{3,2},{4,5},{5,4},{6,7},{7,6},{8,9},{9,8},{10,11... | collective-permute-start | bytes 2654216 | tf_op jit(solution)/shard_map/ppermute | solution.py:140
  70.0 0.5 fusion.3
  70.5 1.7 %collective-permute-done = f32[576,384]{1,0:T(8,128)S(1)} collective-permute-done((f32[576,384]{1,0:T(8,128)}, f32[576,384]{1,0:T(8,128)S(1)}, u32[]{:S(2)}, u32[]{:S(2)}) %collective-permute-start) | collective-permute-done | bytes 884768 | tf_op jit(solution)/shard_map/ppermute | solution.py:140
  72.2 0.7 abs_reduce_fusion
  73.6 0.1 multiply_convert_fusion
  73.7 0.1 concatenate.3
  73.8 22.2 %all_to_all.20 = f16[8,80,384]{2,1,0:T(8,128)(2,1)S(1)} all-to-all(f16[8,80,384]{2,1,0:T(8,128)(2,1)S(1)} %concatenate.3), channel_id=1, replica_groups=mesh['y1'=2,'y0'=2,'z2'=2,'z1'=2,'z0'=2,'y2'=2,'x2'=2,'x1'=2,'x0'=2,'c'=..., dimensions={0} | all-to-all | bytes 983040 | tf_op jit(solution)/shard_map/all_to_all | solution.py:21
  96.0 0.1 multiply_reduce_fusion
  96.1 0.1 divide_convert_fusion
  96.3 15.5 %all_to_all.21 = bf16[8,72,384]{2,1,0:T(8,128)(2,1)S(1)} all-to-all(bf16[8,72,384]{2,1,0:T(8,128)(2,1)S(1)} %broadcast_in_dim.5), channel_id=1, replica_groups=mesh['y1'=2,'y0'=2,'z2'=2,'z1'=2,'z0'=2,'y2'=2,'x2'=2,'x1'=2,'x0'=2,'c'=..., dimensions={0} | all-to-all | bytes 884736 | tf_op jit(solution)/shard_map/all_to_all | solution.py:21
  111.8 5.5 %collective-permute-start.1 = (bf16[576,384]{1,0:T(8,128)(2,1)S(1)}, bf16[576,384]{1,0:T(8,128)(2,1)S(1)}, u32[]{:S(2)}, u32[]{:S(2)}) collective-permute-start(bf16[576,384]{1,0:T(8,128)(2,1)S(1)} %bitcast.17), channel_id=1, source_target_pairs={{0,1},{1,0},{2,3},{3,2},{4,5},{5,4},{6,7},{7,6},{8,9},{9,8},{10,11... | collective-permute-start | bytes 1327112 | tf_op jit(solution)/shard_map/ppermute | solution.py:150
  117.3 0.5 fusion.7
  117.8 0.9 collective-permute-done.1
  118.7 0.5 fusion
  119.2 0.3 copy.12
  119.5 26.5 %all_to_all.22.in_ref = bf16[64,8,576]{2,1,0:T(8,128)(2,1)} all-to-all(bf16[64,8,576]{2,1,0:T(8,128)(2,1)S(1)} %bitcast.16), channel_id=1, replica_groups=mesh['y1'=2,'y0'=2,'z2'=2,'z1'=2,'z0'=2,'y2'=2,'x2'=2,'x1'=2,'x0'=2,'c'=..., dimensions={0} | all-to-all | bytes 1179648 | tf_op jit(solution)/shard_map/all_to_all | solution.py:21
  146.0 2.4 %shard_map.56 = f32[10,8,3072]{2,1,0:T(8,128)} custom-call(s32[3]{0:T(128)} %left_ref.3, bf16[64,8,576]{2,1,0:T(8,128)(2,1)} %all_to_all.22.in_ref), custom_call_target="tpu_custom_call" | custom-call | tf_op jit(solution)/shard_map/pallas_call | solution.py:81
  (5 shorter events, 0.1 us)
Async XLA Ops:
  3.6 25.6 %copy-start = (f32[10]{0:T(128)S(1)}, f32[10]{0:T(128)}, u32[]{:S(2)}) copy-start(f32[10]{0:T(128)} %param.6) | copy-start | bytes 124
  3.6 26.2 %copy-start.1 = (s32[3]{0:T(128)S(1)}, s32[3]{0:T(128)}, u32[]{:S(2)}) copy-start(s32[3]{0:T(128)} %left_ref.3) | copy-start | bytes 40
  3.6 58.8 %all-to-all-start = ((bf16[64,8,1344]{2,1,0:T(8,128)(2,1)}), bf16[64,8,1344]{2,1,0:T(8,128)(2,1)S(1)}, u32[]{:S(2)}, u32[]{:S(2)}) async-start(bf16[64,8,1344]{2,1,0:T(8,128)(2,1)} %shard_map.55), calls=%async_computation | async-start | bytes 2883584 | tf_op jit(solution)/shard_map/all_to_all | solution.py:21
  63.8 8.4 %collective-permute-start = (f32[576,384]{1,0:T(8,128)}, f32[576,384]{1,0:T(8,128)S(1)}, u32[]{:S(2)}, u32[]{:S(2)}) collective-permute-start(f32[576,384]{1,0:T(8,128)} %fusion.1), channel_id=1, source_target_pairs={{0,1},{1,0},{2,3},{3,2},{4,5},{5,4},{6,7},{7,6},{8,9},{9,8},{10,11... | collective-permute-start | bytes 2654216 | tf_op jit(solution)/shard_map/ppermute | solution.py:140
  111.8 6.9 %collective-permute-start.1 = (bf16[576,384]{1,0:T(8,128)(2,1)S(1)}, bf16[576,384]{1,0:T(8,128)(2,1)S(1)}, u32[]{:S(2)}, u32[]{:S(2)}) collective-permute-start(bf16[576,384]{1,0:T(8,128)(2,1)S(1)} %bitcast.17), channel_id=1, source_target_pairs={{0,1},{1,0},{2,3},{3,2},{4,5},{5,4},{6,7},{7,6},{8,9},{9,8},{10,11... | collective-permute-start | bytes 1327112 | tf_op jit(solution)/shard_map/ppermute | solution.py:150

commit v6 on v3

--- a/solution.py
+++ b/solution.py
@@ -88,6 +88,17 @@
     )(left_list, returned)
 
 
+def sum_over_cube(parts):
+    cube, rows, cols = parts.shape
+    largest = jnp.max(jnp.abs(parts))
+    exponent = jnp.clip(14.0 - jnp.ceil(jnp.log2(jnp.maximum(largest, 1e-37))), -100.0, 100.0)
+    scaled = (parts * jnp.exp2(exponent)).astype(jnp.float16)
+    tag = jnp.full((cube, 8, cols), exponent, jnp.float16)
+    got = exchange(jnp.concatenate([scaled, tag], axis=1), A_SUM_BITS)
+    undo = jnp.exp2(-got[:, rows : rows + 1].astype(jnp.float32))
+    return (got[:, :rows].astype(jnp.float32) * undo).sum(axis=0)
+
+
 def body(b_tensor, occ_energy, vir_energy, left_list, right_occ):
     occ_count, rows, virtuals = b_tensor.shape
     pairs = left_list.shape[0]
@@ -129,7 +140,7 @@
     received = lax.ppermute(partial_of(1 - b_sub), B_SUM_BITS, swap)
     own = lax.optimization_barrier(partial_of(b_sub))
     paired = own + received
-    shares = exchange(paired.reshape(a_subs, sub_rows, sub_cols), A_SUM_BITS).sum(axis=0)
+    shares = sum_over_cube(paired.reshape(a_subs, sub_rows, sub_cols))
 
     denominator = row_part[:, None] - vir_b[None, :]
     amp_tile = (shares / denominator).astype(jnp.bfloat16)

time: 156 us -> 153 us (0.981)
  blocking collectives: 60.1 us -> 55.8 us
    all_to_all x3, blocking collectives: 60.1 us -> 55.8 us  [exchange(): return lax.all_to_all(x, axes, split_axis=0, concat_axis=0, tiled=True)]
where the time goes in v6:
time: 153 us; the launch traced here: 152 us
  blocking collectives  55.8 us (36%)
  waiting for transfers between devices  45.3 us (30%)
  starting transfers between devices  36.2 us (24%)
  Pallas kernels  5.29 us (3%)
  local copies, waits for them, and re-layouts  3.43 us (2%)
  matrix products  2.92 us (2%)
  other arithmetic  1.69 us (1%)
  between operations  1.56 us (1%)
    all_to_all x3, blocking collectives, exchange(): return lax.all_to_all(x, axes, split_axis=0, concat_axis=0, tiled=True)  55.8 us
    all_to_all x1, waiting for transfers between devices, exchange(): return lax.all_to_all(x, axes, split_axis=0, concat_axis=0, tiled=True)  42.6 us
    all_to_all x1, starting transfers between devices, exchange(): return lax.all_to_all(x, axes, split_axis=0, concat_axis=0, tiled=True)  28 us
    ppermute x1, starting transfers between devices, body(): other_amps = lax.ppermute(amps, B_SUM_BITS, swap)  4.83 us
    ppermute x1, starting transfers between devices, body(): received = lax.ppermute(partial_of(1 - b_sub), B_SUM_BITS, swap)  3.39 us
  transfers between devices with their start and end apart: 3, of which 3 were waited for; matrix products, arithmetic and copies ran while one was open for 3% of the time, Pallas kernels for 0%

profile of v6, /device:TPU:1, one launch (start us, length us, event | category | flops | bytes accessed | tf_op | source)
XLA Modules:
  0.0 152.1 jit_solution(3929358427677899173)
XLA Ops:
  0.7 2.9 %shard_map.55 = bf16[64,8,1344]{2,1,0:T(8,128)(2,1)} custom-call(s32[3]{0:T(128)} %left_ref.3, s32[1]{0:T(128)} %copy.15.right_ref, bf16[10,8,3072]{2,1,0:T(8,128)(2,1)} %b_ref.1), custom_call_target="tpu_custom_call" | custom-call | tf_op jit(solution)/shard_map/pallas_call | solution.py:48
  3.6 0.0 copy-start
  3.6 0.0 copy-start.1
  3.6 28.0 %all-to-all-start = ((bf16[64,8,1344]{2,1,0:T(8,128)(2,1)}), bf16[64,8,1344]{2,1,0:T(8,128)(2,1)S(1)}, u32[]{:S(2)}, u32[]{:S(2)}) async-start(bf16[64,8,1344]{2,1,0:T(8,128)(2,1)} %shard_map.55), calls=%async_computation | async-start | bytes 2883584 | tf_op jit(solution)/shard_map/all_to_all | solution.py:21
  31.6 0.8 dynamic_slice.21
  32.4 0.8 dynamic_slice.23
  33.2 0.0 copy-done
  33.2 0.6 dynamic_slice.20
  33.7 0.0 copy-done.1
  33.8 0.6 gather_fusion
  34.4 0.6 broadcast_add_fusion
  35.1 0.1 broadcast_subtract_fusion
  35.1 0.1 sub.44
  35.2 0.1 dynamic_slice.22
  35.3 42.6 %all-to-all-done = bf16[64,8,1344]{2,1,0:T(8,128)(2,1)S(1)} async-done(((bf16[64,8,1344]{2,1,0:T(8,128)(2,1)}), bf16[64,8,1344]{2,1,0:T(8,128)(2,1)S(1)}, u32[]{:S(2)}, u32[]{:S(2)}) %all-to-all-start) | async-done | bytes 1376288 | tf_op jit(solution)/shard_map/all_to_all | solution.py:21
  77.9 0.1 slice.18
  78.0 1.4 fusion.1
  79.4 3.4 %collective-permute-start = (f32[576,384]{1,0:T(8,128)}, f32[576,384]{1,0:T(8,128)S(1)}, u32[]{:S(2)}, u32[]{:S(2)}) collective-permute-start(f32[576,384]{1,0:T(8,128)} %fusion.1), channel_id=1, source_target_pairs={{0,1},{1,0},{2,3},{3,2},{4,5},{5,4},{6,7},{7,6},{8,9},{9,8},{10,11... | collective-permute-start | bytes 2654216 | tf_op jit(solution)/shard_map/ppermute | solution.py:140
  82.8 0.5 fusion.3
  83.3 1.7 %collective-permute-done = f32[576,384]{1,0:T(8,128)S(1)} collective-permute-done((f32[576,384]{1,0:T(8,128)}, f32[576,384]{1,0:T(8,128)S(1)}, u32[]{:S(2)}, u32[]{:S(2)}) %collective-permute-start) | collective-permute-done | bytes 884768 | tf_op jit(solution)/shard_map/ppermute | solution.py:140
  85.0 0.7 abs_reduce_fusion
  86.5 0.1 multiply_convert_fusion
  86.6 0.1 concatenate.3
  86.7 11.2 %all_to_all.20 = f16[8,80,384]{2,1,0:T(8,128)(2,1)S(1)} all-to-all(f16[8,80,384]{2,1,0:T(8,128)(2,1)S(1)} %concatenate.3), channel_id=1, replica_groups=mesh['y1'=2,'y0'=2,'z2'=2,'z1'=2,'z0'=2,'y2'=2,'x2'=2,'x1'=2,'x0'=2,'c'=..., dimensions={0} | all-to-all | bytes 983040 | tf_op jit(solution)/shard_map/all_to_all | solution.py:21
  97.9 0.1 multiply_reduce_fusion
  98.0 0.1 divide_convert_fusion
  98.1 9.1 %all_to_all.21 = bf16[8,72,384]{2,1,0:T(8,128)(2,1)S(1)} all-to-all(bf16[8,72,384]{2,1,0:T(8,128)(2,1)S(1)} %broadcast_in_dim.5), channel_id=1, replica_groups=mesh['y1'=2,'y0'=2,'z2'=2,'z1'=2,'z0'=2,'y2'=2,'x2'=2,'x1'=2,'x0'=2,'c'=..., dimensions={0} | all-to-all | bytes 884736 | tf_op jit(solution)/shard_map/all_to_all | solution.py:21
  107.2 4.8 %collective-permute-start.1 = (bf16[576,384]{1,0:T(8,128)(2,1)S(1)}, bf16[576,384]{1,0:T(8,128)(2,1)S(1)}, u32[]{:S(2)}, u32[]{:S(2)}) collective-permute-start(bf16[576,384]{1,0:T(8,128)(2,1)S(1)} %bitcast.17), channel_id=1, source_target_pairs={{0,1},{1,0},{2,3},{3,2},{4,5},{5,4},{6,7},{7,6},{8,9},{9,8},{10,11... | collective-permute-start | bytes 1327112 | tf_op jit(solution)/shard_map/ppermute | solution.py:150
  112.0 0.5 fusion.7
  112.5 0.9 collective-permute-done.1
  113.4 0.5 fusion
  113.9 0.3 copy.12
  114.2 35.5 %all_to_all.22.in_ref = bf16[64,8,576]{2,1,0:T(8,128)(2,1)} all-to-all(bf16[64,8,576]{2,1,0:T(8,128)(2,1)S(1)} %bitcast.16), channel_id=1, replica_groups=mesh['y1'=2,'y0'=2,'z2'=2,'z1'=2,'z0'=2,'y2'=2,'x2'=2,'x1'=2,'x0'=2,'c'=..., dimensions={0} | all-to-all | bytes 1179648 | tf_op jit(solution)/shard_map/all_to_all | solution.py:21
  149.8 2.4 %shard_map.56 = f32[10,8,3072]{2,1,0:T(8,128)} custom-call(s32[3]{0:T(128)} %left_ref.3, bf16[64,8,576]{2,1,0:T(8,128)(2,1)} %all_to_all.22.in_ref), custom_call_target="tpu_custom_call" | custom-call | tf_op jit(solution)/shard_map/pallas_call | solution.py:81
  (5 shorter events, 0.1 us)
Async XLA Ops:
  3.6 29.6 %copy-start = (f32[10]{0:T(128)S(1)}, f32[10]{0:T(128)}, u32[]{:S(2)}) copy-start(f32[10]{0:T(128)} %param.6) | copy-start | bytes 124
  3.6 30.2 %copy-start.1 = (s32[3]{0:T(128)S(1)}, s32[3]{0:T(128)}, u32[]{:S(2)}) copy-start(s32[3]{0:T(128)} %left_ref.3) | copy-start | bytes 40
  3.6 74.3 %all-to-all-start = ((bf16[64,8,1344]{2,1,0:T(8,128)(2,1)}), bf16[64,8,1344]{2,1,0:T(8,128)(2,1)S(1)}, u32[]{:S(2)}, u32[]{:S(2)}) async-start(bf16[64,8,1344]{2,1,0:T(8,128)(2,1)} %shard_map.55), calls=%async_computation | async-start | bytes 2883584 | tf_op jit(solution)/shard_map/all_to_all | solution.py:21
  79.4 5.6 %collective-permute-start = (f32[576,384]{1,0:T(8,128)}, f32[576,384]{1,0:T(8,128)S(1)}, u32[]{:S(2)}, u32[]{:S(2)}) collective-permute-start(f32[576,384]{1,0:T(8,128)} %fusion.1), channel_id=1, source_target_pairs={{0,1},{1,0},{2,3},{3,2},{4,5},{5,4},{6,7},{7,6},{8,9},{9,8},{10,11... | collective-permute-start | bytes 2654216 | tf_op jit(solution)/shard_map/ppermute | solution.py:140
  107.2 6.2 %collective-permute-start.1 = (bf16[576,384]{1,0:T(8,128)(2,1)S(1)}, bf16[576,384]{1,0:T(8,128)(2,1)S(1)}, u32[]{:S(2)}, u32[]{:S(2)}) collective-permute-start(bf16[576,384]{1,0:T(8,128)(2,1)S(1)} %bitcast.17), channel_id=1, source_target_pairs={{0,1},{1,0},{2,3},{3,2},{4,5},{5,4},{6,7},{7,6},{8,9},{9,8},{10,11... | collective-permute-start | bytes 1327112 | tf_op jit(solution)/shard_map/ppermute | solution.py:150

commit v7 on v5

--- a/solution.py
+++ b/solution.py
@@ -65,27 +65,63 @@
     a_width = pa_width // pairs
     virtuals = a_parts * a_width
 
-    def kernel(left_ref, in_ref, out_ref, rows_ref):
+    def kernel(left_ref, in_ref, out_ref, rows_ref, made_ref, sems):
         for a in range(a_parts):
             total = in_ref[a * b_parts].astype(jnp.float32)
             for b in range(1, b_parts):
                 total = total + in_ref[a * b_parts + b].astype(jnp.float32)
             for p in range(pairs):
                 rows_ref[p, :, a * a_width : (a + 1) * a_width] = total[:, p * a_width : (p + 1) * a_width]
+        copies = []
         for orbital in range(occ_count):
             total = jnp.zeros((rows, virtuals), jnp.float32)
             for p in range(pairs):
                 total = total + jnp.where(left_ref[p] == orbital, rows_ref[p], 0.0)
-            out_ref[orbital] = total
+            made_ref[orbital] = total
+            copies.append(pltpu.make_async_copy(made_ref.at[orbital], out_ref.at[orbital], sems.at[orbital]))
+            copies[-1].start()
+        for copy in copies:
+            copy.wait()
 
     return pl.pallas_call(
         kernel,
         out_shape=jax.ShapeDtypeStruct((occ_count, rows, virtuals), jnp.float32),
         in_specs=[pl.BlockSpec(memory_space=pltpu.SMEM), pl.BlockSpec(memory_space=pltpu.VMEM)],
-        out_specs=pl.BlockSpec(memory_space=pltpu.VMEM),
-        scratch_shapes=[pltpu.VMEM((pairs, rows, virtuals), jnp.float32)],
+        out_specs=pl.BlockSpec(memory_space=pl.ANY),
+        scratch_shapes=[
+            pltpu.VMEM((pairs, rows, virtuals), jnp.float32),
+            pltpu.VMEM((occ_count, rows, virtuals), jnp.float32),
+            pltpu.SemaphoreType.DMA((occ_count,)),
+        ],
         interpret=INTERPRET,
     )(left_list, returned)
+
+
+def make_denominator(place, left_list, right_occ, occ_energy, vir_energy, shape, a_width):
+    rows, cols = shape
+    pairs, virtuals = left_list.shape[0], vir_energy.shape[0]
+
+    def kernel(place_ref, left_ref, right_ref, occ_ref, vir_ref, out_ref):
+        row = place_ref[1] + lax.broadcasted_iota(jnp.int32, (rows, 1), 0)
+        shift = jnp.zeros((rows, 1), jnp.float32)
+        column = place_ref[0] + row
+        for p in range(pairs):
+            here = (row >= p * a_width) & (row < (p + 1) * a_width)
+            shift = jnp.where(here, occ_ref[left_ref[p]] + occ_ref[right_ref[0]], shift)
+            column = jnp.where(here, place_ref[0] + row - p * a_width, column)
+        lanes = lax.broadcasted_iota(jnp.int32, (rows, virtuals), 1)
+        vir_a = jnp.sum(jnp.where(lanes == column, vir_ref[...], 0.0), axis=1, keepdims=True)
+        vir_b = vir_ref[:, pl.ds(pl.multiple_of(place_ref[2], 128), cols)]
+        out_ref[...] = (shift - vir_a) - vir_b
+
+    smem = pl.BlockSpec(memory_space=pltpu.SMEM)
+    return pl.pallas_call(
+        kernel,
+        out_shape=jax.ShapeDtypeStruct(shape, jnp.float32),
+        in_specs=[smem, smem, smem, smem, pl.BlockSpec(memory_space=pltpu.VMEM)],
+        out_specs=pl.BlockSpec(memory_space=pltpu.VMEM),
+        interpret=INTERPRET,
+    )(place, left_list, right_occ, occ_energy, vir_energy.reshape(1, virtuals))
 
 
 def sum_over_ring(parts):
@@ -110,39 +146,40 @@
     peers = a_parts * b_parts
     group_rows = peers * rows
 
-    second_occ = right_occ[0]
-    packed = pack_rows(left_list, right_occ, b_tensor, a_parts, b_parts)
-    got = exchange(packed, AB_BITS)
-
     b_sub = lax.axis_index(B_SUM_BITS)
     a_rank, b_rank = lax.axis_index(A_BITS), lax.axis_index(B_BITS)
     a_sub = lax.axis_index(A_SUM_BITS)
-    vir_a = lax.dynamic_slice_in_dim(vir_energy, a_rank * a_width, a_width)
-    shift = occ_energy[left_list] + occ_energy[second_occ]
-    row_part = (shift[:, None] - vir_a[None, :]).reshape(pa_width)
-    row_part = lax.dynamic_slice_in_dim(row_part, a_sub * sub_rows, sub_rows)
-    vir_b = lax.dynamic_slice_in_dim(vir_energy, b_rank * b_width + b_sub * sub_cols, sub_cols)
-    got, row_part, vir_b = lax.optimization_barrier((got, row_part, vir_b))
-
+    place = (a_rank * a_width, a_sub * sub_rows, b_rank * b_width + b_sub * sub_cols)
+    own_start = (b_sub * sub_cols).astype(jnp.uint32)
+    other_start = ((1 - b_sub) * sub_cols).astype(jnp.uint32)
+
+    packed = pack_rows(left_list, right_occ, b_tensor, a_parts, b_parts)
+    packed, place, own_start, other_start = lax.optimization_barrier((packed, place, own_start, other_start))
+    got = exchange(packed, AB_BITS)
     got = got.reshape(group_rows, b_width + pa_width)
     right = got[:, :b_width]
     left = got[:, b_width:]
 
-    def half_of(half):
-        return lax.dynamic_slice_in_dim(right, half * sub_cols, sub_cols, axis=1)
+    def half_of(start):
+        return lax.dynamic_slice(right, (jnp.uint32(0), start), (group_rows, sub_cols))
 
     swap = [(0, 1), (1, 0)]
 
-    def partial_of(half):
-        cols = half_of(half)
+    def partial_of(start):
+        cols = half_of(start)
         return lax.dot_general(left, cols, (((0,), (0,)), ((), ())), preferred_element_type=jnp.float32)
 
-    received = lax.ppermute(partial_of(1 - b_sub), B_SUM_BITS, swap)
-    own = lax.optimization_barrier(partial_of(b_sub))
+    first = partial_of(other_start)
+    received = lax.ppermute(first, B_SUM_BITS, swap)
+    place, _ = lax.optimization_barrier((place, first))
+    denominator = make_denominator(
+        jnp.stack(place), left_list, right_occ, occ_energy, vir_energy, (sub_rows, sub_cols), a_width
+    )
+    own = partial_of(own_start)
+    own, denominator = lax.optimization_barrier((own, denominator))
     paired = own + received
     shares = sum_over_ring(paired.reshape(a_subs, sub_rows, sub_cols))
 
-    denominator = row_part[:, None] - vir_b[None, :]
     amp_tile = (shares / denominator).astype(jnp.bfloat16)
 
     amps = exchange(jnp.broadcast_to(amp_tile[None], (a_subs, sub_rows, sub_cols)), A_SUM_BITS)
@@ -152,8 +189,8 @@
     def contribution(cols, amp_cols):
         return lax.dot_general(cols, amp_cols, (((1,), (1,)), ((), ())), preferred_element_type=jnp.float32)
 
-    own = lax.optimization_barrier(contribution(half_of(b_sub), amps))
-    contrib = own + contribution(half_of(1 - b_sub), other_amps)
+    own = lax.optimization_barrier(contribution(half_of(own_start), amps))
+    contrib = own + contribution(half_of(other_start), other_amps)
     returned = exchange(contrib.reshape(peers, rows, pa_width).astype(jnp.bfloat16), AB_BITS)
     return place_rows(left_list, returned, occ_count, a_parts, b_parts)
 

time: 151 us -> 153 us (1.013)
  blocking collectives: 64.2 us -> 127 us
  waiting for transfers between devices: 33.7 us -> 0.81 us
  starting transfers between devices: 35.6 us -> 8.59 us
  local copies, waits for them, and re-layouts: 3.43 us -> 0.49 us
  Pallas kernels: 5.29 us -> 6.89 us
    all_to_all x3 -> x4, blocking collectives: 64.2 us -> 127 us  [exchange(): return lax.all_to_all(x, axes, split_axis=0, concat_axis=0, tiled=True)]
    all_to_all x1 -> x0, waiting for transfers between devices: 31.1 us -> none  [exchange(): return lax.all_to_all(x, axes, split_axis=0, concat_axis=0, tiled=True)]
    all_to_all x1 -> x0, starting transfers between devices: 24 us -> none  [exchange(): return lax.all_to_all(x, axes, split_axis=0, concat_axis=0, tiled=True)]
    ppermute x1, starting transfers between devices: 5.46 us -> 2.47 us  [body(): other_amps = lax.ppermute(amps, B_SUM_BITS, swap)]
    dynamic_slice x4 -> x0, local copies, waits for them, and re-layouts: 2.21 us -> none  [the longest x1 0.78 us: body(): vir_a = lax.dynamic_slice_in_dim(vir_energy, a_rank * a_width, a_width)]
    ppermute x1, waiting for transfers between devices: 1.74 us -> 0.01 us  [body(): received = lax.ppermute(first, B_SUM_BITS, swap)]
    pallas_call x0 -> x1, Pallas kernels: none -> 1.57 us  [make_denominator(): pl.pallas_call(kernel, out_shape=jax.ShapeDtypeStruct(shape, jnp.float32)...]
  transfers between devices with their start and end apart: 3 -> 2, of which waited for: 3 -> 1; matrix products, arithmetic and copies ran while one was open for 3% -> 1% of each run, Pallas kernels for 0% -> 1%
where the time goes in v7:
time: 153 us; the launch traced here: 150 us
  blocking collectives  127 us (83%)
  starting transfers between devices  8.59 us (6%)
  Pallas kernels  6.89 us (5%)
  matrix products  3.22 us (2%)
  other arithmetic  1.57 us (1%)
    all_to_all x4, blocking collectives, exchange(): return lax.all_to_all(x, axes, split_axis=0, concat_axis=0, tiled=True)  127 us
    ppermute x1, starting transfers between devices, body(): received = lax.ppermute(first, B_SUM_BITS, swap)  6.11 us
  transfers between devices with their start and end apart: 2, of which 1 were waited for; matrix products, arithmetic and copies ran while one was open for 1% of the time, Pallas kernels for 1%

profile of v7, /device:TPU:1, one launch (start us, length us, event | category | flops | bytes accessed | tf_op | source)
XLA Modules:
  0.0 150.4 jit_solution(9455694887646298594)
XLA Ops:
  0.7 2.9 %shard_map.55 = bf16[64,8,1344]{2,1,0:T(8,128)(2,1)} custom-call(s32[3]{0:T(128)} %left_ref.5, s32[1]{0:T(128)S(6)} %copy.14.right_ref, bf16[10,8,3072]{2,1,0:T(8,128)(2,1)} %b_ref.1), custom_call_target="tpu_custom_call" | custom-call | tf_op jit(solution)/shard_map/pallas_call | solution.py:48
  3.6 58.7 %all_to_all.20 = bf16[64,8,1344]{2,1,0:T(8,128)(2,1)S(1)} all-to-all(bf16[64,8,1344]{2,1,0:T(8,128)(2,1)} %shard_map.55), channel_id=1, replica_groups=mesh['y1'=2,'y0'=2,'z2'=2,'z1'=2,'z0'=2,'y2'=2,'x2'=2,'x1'=2,'x0'=2,'c'=..., dimensions={0} | all-to-all | bytes 2752512 | tf_op jit(solution)/shard_map/all_to_all | solution.py:21
  62.3 0.1 slice.16
  62.4 1.5 fusion.1
  63.9 6.1 %collective-permute-start = (f32[576,384]{1,0:T(8,128)}, f32[576,384]{1,0:T(8,128)S(1)}, u32[]{:S(2)}, u32[]{:S(2)}) collective-permute-start(f32[576,384]{1,0:T(8,128)} %fusion.1), channel_id=1, source_target_pairs={{0,1},{1,0},{2,3},{3,2},{4,5},{5,4},{6,7},{7,6},{8,9},{9,8},{10,11... | collective-permute-start | bytes 2654216 | tf_op jit(solution)/shard_map/ppermute | solution.py:173
  70.0 0.7 pad_add_fusion.place_ref
  70.7 1.6 %shard_map.56 = f32[72,384]{1,0:T(8,128)} custom-call(s32[3]{0:T(128)} %pad_add_fusion.place_ref, s32[3]{0:T(128)} %left_ref.5, s32[1]{0:T(128)S(6)} %copy.14.right_ref, f32[10]{0:T(128)} %occ_ref.1, f32[1,3072]{1,0:T(1,128)} %bitcast.19), custom_call_target="tpu_custom_call" | custom-call | tf_op jit(solution)/shard_map/pallas_call | solution.py:118
  72.2 0.6 fusion.3
  72.8 0.0 collective-permute-done
  72.8 0.7 abs_reduce_fusion
  74.3 0.1 multiply_convert_fusion
  74.3 0.0 copy-start
  74.4 0.1 concatenate.3
  74.4 23.6 %all_to_all.21 = f16[8,80,384]{2,1,0:T(8,128)(2,1)S(1)} all-to-all(f16[8,80,384]{2,1,0:T(8,128)(2,1)S(1)} %concatenate.3), channel_id=1, replica_groups=mesh['y1'=2,'y0'=2,'z2'=2,'z1'=2,'z0'=2,'y2'=2,'x2'=2,'x1'=2,'x0'=2,'c'=..., dimensions={0} | all-to-all | bytes 983040 | tf_op jit(solution)/shard_map/all_to_all | solution.py:21
  98.0 0.1 multiply_reduce_fusion
  98.1 0.0 copy-done
  98.2 18.5 %all_to_all.22 = bf16[8,72,384]{2,1,0:T(8,128)(2,1)S(1)} all-to-all(bf16[8,72,384]{2,1,0:T(8,128)(2,1)S(1)} %broadcast_in_dim.2), channel_id=1, replica_groups=mesh['y1'=2,'y0'=2,'z2'=2,'z1'=2,'z0'=2,'y2'=2,'x2'=2,'x1'=2,'x0'=2,'c'=..., dimensions={0} | all-to-all | bytes 884736 | tf_op jit(solution)/shard_map/all_to_all | solution.py:21
  116.7 2.5 %collective-permute-start.1 = (bf16[576,384]{1,0:T(8,128)(2,1)S(1)}, bf16[576,384]{1,0:T(8,128)(2,1)S(1)}, u32[]{:S(2)}, u32[]{:S(2)}) collective-permute-start(bf16[576,384]{1,0:T(8,128)(2,1)S(1)} %bitcast.16), channel_id=1, source_target_pairs={{0,1},{1,0},{2,3},{3,2},{4,5},{5,4},{6,7},{7,6},{8,9},{9,8},{10,11... | collective-permute-start | bytes 1327112 | tf_op jit(solution)/shard_map/ppermute | solution.py:187
  119.2 0.6 fusion.7
  119.8 0.8 collective-permute-done.1
  120.6 0.6 fusion
  121.2 0.3 copy.11
  121.5 26.5 %all_to_all.23.in_ref = bf16[64,8,576]{2,1,0:T(8,128)(2,1)} all-to-all(bf16[64,8,576]{2,1,0:T(8,128)(2,1)S(1)} %bitcast.15), channel_id=1, replica_groups=mesh['y1'=2,'y0'=2,'z2'=2,'z1'=2,'z0'=2,'y2'=2,'x2'=2,'x1'=2,'x0'=2,'c'=..., dimensions={0} | all-to-all | bytes 1179648 | tf_op jit(solution)/shard_map/all_to_all | solution.py:21
  148.0 2.4 %shard_map.57 = f32[10,8,3072]{2,1,0:T(8,128)} custom-call(s32[3]{0:T(128)} %left_ref.5, bf16[64,8,576]{2,1,0:T(8,128)(2,1)} %all_to_all.23.in_ref), custom_call_target="tpu_custom_call" | custom-call | tf_op jit(solution)/shard_map/pallas_call | solution.py:86
  (4 shorter events, 0.1 us)
Async XLA Ops:
  63.9 8.9 %collective-permute-start = (f32[576,384]{1,0:T(8,128)}, f32[576,384]{1,0:T(8,128)S(1)}, u32[]{:S(2)}, u32[]{:S(2)}) collective-permute-start(f32[576,384]{1,0:T(8,128)} %fusion.1), channel_id=1, source_target_pairs={{0,1},{1,0},{2,3},{3,2},{4,5},{5,4},{6,7},{7,6},{8,9},{9,8},{10,11... | collective-permute-start | bytes 2654216 | tf_op jit(solution)/shard_map/ppermute | solution.py:173
  74.3 23.8 %copy-start = (f32[72,384]{1,0:T(8,128)S(1)}, f32[72,384]{1,0:T(8,128)}, u32[]{:S(2)}) copy-start(f32[72,384]{1,0:T(8,128)} %shard_map.56) | copy-start | bytes 331780
  116.7 3.9 %collective-permute-start.1 = (bf16[576,384]{1,0:T(8,128)(2,1)S(1)}, bf16[576,384]{1,0:T(8,128)(2,1)S(1)}, u32[]{:S(2)}, u32[]{:S(2)}) collective-permute-start(bf16[576,384]{1,0:T(8,128)(2,1)S(1)} %bitcast.16), channel_id=1, source_target_pairs={{0,1},{1,0},{2,3},{3,2},{4,5},{5,4},{6,7},{7,6},{8,9},{9,8},{10,11... | collective-permute-start | bytes 1327112 | tf_op jit(solution)/shard_map/ppermute | solution.py:187

commit v8 on v7

--- a/solution.py
+++ b/solution.py
@@ -47,7 +47,7 @@
 
     return pl.pallas_call(
         kernel,
-        out_shape=jax.ShapeDtypeStruct((a_parts * b_parts, rows, b_width + pairs * a_width), b_tensor.dtype),
+        out_shape=pltpu.VMEM((a_parts * b_parts, rows, b_width + pairs * a_width), b_tensor.dtype),
         in_specs=[
             pl.BlockSpec(memory_space=pltpu.SMEM),
             pl.BlockSpec(memory_space=pltpu.SMEM),
@@ -192,6 +192,7 @@
     own = lax.optimization_barrier(contribution(half_of(own_start), amps))
     contrib = own + contribution(half_of(other_start), other_amps)
     returned = exchange(contrib.reshape(peers, rows, pa_width).astype(jnp.bfloat16), AB_BITS)
+    returned = pltpu.with_memory_space_constraint(returned, pltpu.VMEM)
     return place_rows(left_list, returned, occ_count, a_parts, b_parts)
 
 

time: 153 us -> 153 us (level)
  Pallas kernels: 6.89 us -> 5.35 us
where the time goes in v8:
time: 153 us; the launch traced here: 150 us
  blocking collectives  127 us (83%)
  starting transfers between devices  8.59 us (6%)
  Pallas kernels  5.35 us (3%)
  matrix products  3.22 us (2%)
  other arithmetic  2.63 us (2%)
    all_to_all x4, blocking collectives, exchange(): return lax.all_to_all(x, axes, split_axis=0, concat_axis=0, tiled=True)  127 us
    ppermute x1, starting transfers between devices, body(): received = lax.ppermute(first, B_SUM_BITS, swap)  6.12 us
  transfers between devices with their start and end apart: 2, of which 1 were waited for; matrix products, arithmetic and copies ran while one was open for 1% of the time, Pallas kernels for 1%

profile of v8, /device:TPU:1, one launch (start us, length us, event | category | flops | bytes accessed | tf_op | source)
XLA Modules:
  0.0 149.6 jit_solution(11804400659935615471)
XLA Ops:
  0.7 1.8 %shard_map.55 = bf16[64,8,1344]{2,1,0:T(8,128)(2,1)S(1)} custom-call(s32[3]{0:T(128)} %left_ref.5, s32[1]{0:T(128)S(6)} %copy.14.right_ref, bf16[10,8,3072]{2,1,0:T(8,128)(2,1)} %b_ref.1), custom_call_target="tpu_custom_call" | custom-call | tf_op jit(solution)/shard_map/pallas_call | solution.py:48
  2.5 58.5 %all_to_all.20 = bf16[64,8,1344]{2,1,0:T(8,128)(2,1)S(1)} all-to-all(bf16[64,8,1344]{2,1,0:T(8,128)(2,1)S(1)} %shard_map.55), channel_id=1, replica_groups=mesh['y1'=2,'y0'=2,'z2'=2,'z1'=2,'z0'=2,'y2'=2,'x2'=2,'x1'=2,'x0'=2,'c'=..., dimensions={0} | all-to-all | bytes 2752512 | tf_op jit(solution)/shard_map/all_to_all | solution.py:21
  61.0 0.1 slice.16
  61.0 1.5 fusion.1
  62.5 6.1 %collective-permute-start = (f32[576,384]{1,0:T(8,128)}, f32[576,384]{1,0:T(8,128)}, u32[]{:S(2)}, u32[]{:S(2)}) collective-permute-start(f32[576,384]{1,0:T(8,128)} %fusion.1), channel_id=1, source_target_pairs={{0,1},{1,0},{2,3},{3,2},{4,5},{5,4},{6,7},{7,6},{8,9},{9,8},{10,11... | collective-permute-start | bytes 2654216 | tf_op jit(solution)/shard_map/ppermute | solution.py:173
  68.7 0.6 pad_add_fusion.place_ref
  69.2 1.6 %shard_map.56 = f32[72,384]{1,0:T(8,128)} custom-call(s32[3]{0:T(128)} %pad_add_fusion.place_ref, s32[3]{0:T(128)} %left_ref.5, s32[1]{0:T(128)S(6)} %copy.14.right_ref, f32[10]{0:T(128)} %occ_ref.1, f32[1,3072]{1,0:T(1,128)} %bitcast.19), custom_call_target="tpu_custom_call" | custom-call | tf_op jit(solution)/shard_map/pallas_call | solution.py:118
  70.8 0.6 fusion.3
  71.4 0.0 collective-permute-done
  71.4 1.9 %abs_reduce_fusion = (f32[]{:T(128)}, f32[576,384]{1,0:T(8,128)S(1)}) fusion(f32[576,384]{1,0:T(8,128)S(1)} %fusion.3, f32[576,384]{1,0:T(8,128)} %collective-permute-done), kind=kLoop, calls=%fused_computation.4 | loop fusion | flops 663551 | bytes 2654212 | tf_op jit(solution)/shard_map/reduce_max | solution.py:129
  74.0 0.1 multiply_convert_fusion
  74.1 0.0 copy-start
  74.1 0.1 concatenate.3
  74.2 23.6 %all_to_all.21 = f16[8,80,384]{2,1,0:T(8,128)(2,1)S(1)} all-to-all(f16[8,80,384]{2,1,0:T(8,128)(2,1)S(1)} %concatenate.3), channel_id=1, replica_groups=mesh['y1'=2,'y0'=2,'z2'=2,'z1'=2,'z0'=2,'y2'=2,'x2'=2,'x1'=2,'x0'=2,'c'=..., dimensions={0} | all-to-all | bytes 983040 | tf_op jit(solution)/shard_map/all_to_all | solution.py:21
  97.8 0.1 multiply_reduce_fusion
  97.9 0.0 copy-done
  98.0 18.5 %all_to_all.22 = bf16[8,72,384]{2,1,0:T(8,128)(2,1)S(1)} all-to-all(bf16[8,72,384]{2,1,0:T(8,128)(2,1)S(1)} %broadcast_in_dim.2), channel_id=1, replica_groups=mesh['y1'=2,'y0'=2,'z2'=2,'z1'=2,'z0'=2,'y2'=2,'x2'=2,'x1'=2,'x0'=2,'c'=..., dimensions={0} | all-to-all | bytes 884736 | tf_op jit(solution)/shard_map/all_to_all | solution.py:21
  116.5 2.5 %collective-permute-start.1 = (bf16[576,384]{1,0:T(8,128)(2,1)S(1)}, bf16[576,384]{1,0:T(8,128)(2,1)S(1)}, u32[]{:S(2)}, u32[]{:S(2)}) collective-permute-start(bf16[576,384]{1,0:T(8,128)(2,1)S(1)} %bitcast.16), channel_id=1, source_target_pairs={{0,1},{1,0},{2,3},{3,2},{4,5},{5,4},{6,7},{7,6},{8,9},{9,8},{10,11... | collective-permute-start | bytes 1327112 | tf_op jit(solution)/shard_map/ppermute | solution.py:187
  119.0 0.6 fusion.7
  119.5 0.8 collective-permute-done.1
  120.4 0.6 fusion
  120.9 0.3 copy.11
  121.2 26.4 %all_to_all.23.in_ref = bf16[64,8,576]{2,1,0:T(8,128)(2,1)S(1)} all-to-all(bf16[64,8,576]{2,1,0:T(8,128)(2,1)S(1)} %bitcast.15), channel_id=1, replica_groups=mesh['y1'=2,'y0'=2,'z2'=2,'z1'=2,'z0'=2,'y2'=2,'x2'=2,'x1'=2,'x0'=2,'c'=..., dimensions={0} | all-to-all | bytes 1179648 | tf_op jit(solution)/shard_map/all_to_all | solution.py:21
  147.6 2.0 %shard_map.57 = f32[10,8,3072]{2,1,0:T(8,128)} custom-call(s32[3]{0:T(128)} %left_ref.5, bf16[64,8,576]{2,1,0:T(8,128)(2,1)S(1)} %all_to_all.23.in_ref), custom_call_target="tpu_custom_call" | custom-call | tf_op jit(solution)/shard_map/pallas_call | solution.py:86
  (4 shorter events, 0.1 us)
Async XLA Ops:
  62.5 8.8 %collective-permute-start = (f32[576,384]{1,0:T(8,128)}, f32[576,384]{1,0:T(8,128)}, u32[]{:S(2)}, u32[]{:S(2)}) collective-permute-start(f32[576,384]{1,0:T(8,128)} %fusion.1), channel_id=1, source_target_pairs={{0,1},{1,0},{2,3},{3,2},{4,5},{5,4},{6,7},{7,6},{8,9},{9,8},{10,11... | collective-permute-start | bytes 2654216 | tf_op jit(solution)/shard_map/ppermute | solution.py:173
  74.1 23.8 %copy-start = (f32[72,384]{1,0:T(8,128)S(1)}, f32[72,384]{1,0:T(8,128)}, u32[]{:S(2)}) copy-start(f32[72,384]{1,0:T(8,128)} %shard_map.56) | copy-start | bytes 331780
  116.5 3.9 %collective-permute-start.1 = (bf16[576,384]{1,0:T(8,128)(2,1)S(1)}, bf16[576,384]{1,0:T(8,128)(2,1)S(1)}, u32[]{:S(2)}, u32[]{:S(2)}) collective-permute-start(bf16[576,384]{1,0:T(8,128)(2,1)S(1)} %bitcast.16), channel_id=1, source_target_pairs={{0,1},{1,0},{2,3},{3,2},{4,5},{5,4},{6,7},{7,6},{8,9},{9,8},{10,11... | collective-permute-start | bytes 1327112 | tf_op jit(solution)/shard_map/ppermute | solution.py:187

commit v9 on v5

--- a/solution.py
+++ b/solution.py
@@ -65,35 +65,44 @@
     a_width = pa_width // pairs
     virtuals = a_parts * a_width
 
-    def kernel(left_ref, in_ref, out_ref, rows_ref):
+    def kernel(left_ref, in_ref, out_ref, rows_ref, made_ref, sems):
         for a in range(a_parts):
             total = in_ref[a * b_parts].astype(jnp.float32)
             for b in range(1, b_parts):
                 total = total + in_ref[a * b_parts + b].astype(jnp.float32)
             for p in range(pairs):
                 rows_ref[p, :, a * a_width : (a + 1) * a_width] = total[:, p * a_width : (p + 1) * a_width]
+        copies = []
         for orbital in range(occ_count):
             total = jnp.zeros((rows, virtuals), jnp.float32)
             for p in range(pairs):
                 total = total + jnp.where(left_ref[p] == orbital, rows_ref[p], 0.0)
-            out_ref[orbital] = total
+            made_ref[orbital] = total
+            copies.append(pltpu.make_async_copy(made_ref.at[orbital], out_ref.at[orbital], sems.at[orbital]))
+            copies[-1].start()
+        for copy in copies:
+            copy.wait()
 
     return pl.pallas_call(
         kernel,
         out_shape=jax.ShapeDtypeStruct((occ_count, rows, virtuals), jnp.float32),
         in_specs=[pl.BlockSpec(memory_space=pltpu.SMEM), pl.BlockSpec(memory_space=pltpu.VMEM)],
-        out_specs=pl.BlockSpec(memory_space=pltpu.VMEM),
-        scratch_shapes=[pltpu.VMEM((pairs, rows, virtuals), jnp.float32)],
+        out_specs=pl.BlockSpec(memory_space=pl.ANY),
+        scratch_shapes=[
+            pltpu.VMEM((pairs, rows, virtuals), jnp.float32),
+            pltpu.VMEM((occ_count, rows, virtuals), jnp.float32),
+            pltpu.SemaphoreType.DMA((occ_count,)),
+        ],
         interpret=INTERPRET,
     )(left_list, returned)
 
 
 def sum_over_ring(parts):
     ring, rows, cols = parts.shape
-    largest = jnp.max(jnp.abs(parts))
+    largest = jnp.max(jnp.abs(parts), axis=(0, 1))
     exponent = jnp.clip(14.0 - jnp.ceil(jnp.log2(jnp.maximum(largest, 1e-37))), -100.0, 100.0)
     scaled = (parts * jnp.exp2(exponent)).astype(jnp.float16)
-    tag = jnp.full((ring, 8, cols), exponent, jnp.float16)
+    tag = jnp.broadcast_to(exponent.astype(jnp.float16), (ring, 8, cols))
     got = exchange(jnp.concatenate([scaled, tag], axis=1), A_SUM_BITS)
     undo = jnp.exp2(-got[:, rows : rows + 1].astype(jnp.float32))
     return (got[:, :rows].astype(jnp.float32) * undo).sum(axis=0)
@@ -155,6 +164,7 @@
     own = lax.optimization_barrier(contribution(half_of(b_sub), amps))
     contrib = own + contribution(half_of(1 - b_sub), other_amps)
     returned = exchange(contrib.reshape(peers, rows, pa_width).astype(jnp.bfloat16), AB_BITS)
+    returned = pltpu.with_memory_space_constraint(returned, pltpu.VMEM)
     return place_rows(left_list, returned, occ_count, a_parts, b_parts)
 
 

time: 151 us -> 150 us (level)
  no operation moved by 1% of the time
where the time goes in v9:
time: 150 us; the launch traced here: 147 us
  blocking collectives  64.1 us (43%)
  starting transfers between devices  35.5 us (24%)
  waiting for transfers between devices  33.7 us (22%)
  Pallas kernels  4.91 us (3%)
  local copies, waits for them, and re-layouts  3.35 us (2%)
  matrix products  2.93 us (2%)
    all_to_all x3, blocking collectives, exchange(): return lax.all_to_all(x, axes, split_axis=0, concat_axis=0, tiled=True)  64.1 us
    all_to_all x1, waiting for transfers between devices, exchange(): return lax.all_to_all(x, axes, split_axis=0, concat_axis=0, tiled=True)  31.1 us
    all_to_all x1, starting transfers between devices, exchange(): return lax.all_to_all(x, axes, split_axis=0, concat_axis=0, tiled=True)  24 us
    ppermute x1, starting transfers between devices, body(): received = lax.ppermute(partial_of(1 - b_sub), B_SUM_BITS, swap)  6.1 us
    ppermute x1, starting transfers between devices, body(): other_amps = lax.ppermute(amps, B_SUM_BITS, swap)  5.46 us
  transfers between devices with their start and end apart: 3, of which 3 were waited for; matrix products, arithmetic and copies ran while one was open for 3% of the time, Pallas kernels for 0%

profile of v9, /device:TPU:1, one launch (start us, length us, event | category | flops | bytes accessed | tf_op | source)
XLA Modules:
  0.0 146.6 jit_solution(220606417468253383)
XLA Ops:
  0.7 2.9 %shard_map.55 = bf16[64,8,1344]{2,1,0:T(8,128)(2,1)} custom-call(s32[3]{0:T(128)} %left_ref.3, s32[1]{0:T(128)} %copy.15.right_ref, bf16[10,8,3072]{2,1,0:T(8,128)(2,1)} %b_ref.1), custom_call_target="tpu_custom_call" | custom-call | tf_op jit(solution)/shard_map/pallas_call | solution.py:48
  3.6 0.0 copy-start
  3.6 0.0 copy-start.1
  3.6 24.0 %all-to-all-start = ((bf16[64,8,1344]{2,1,0:T(8,128)(2,1)}), bf16[64,8,1344]{2,1,0:T(8,128)(2,1)S(1)}, u32[]{:S(2)}, u32[]{:S(2)}) async-start(bf16[64,8,1344]{2,1,0:T(8,128)(2,1)} %shard_map.55), calls=%async_computation | async-start | bytes 2883584 | tf_op jit(solution)/shard_map/all_to_all | solution.py:21
  27.6 0.8 dynamic_slice.21
  28.4 0.8 dynamic_slice.23
  29.2 0.0 copy-done
  29.2 0.6 dynamic_slice.20
  29.8 0.0 copy-done.1
  29.8 0.6 gather_fusion
  30.4 0.6 broadcast_add_fusion
  31.1 0.1 broadcast_subtract_fusion
  31.1 0.1 sub.51
  31.2 0.1 dynamic_slice.22
  31.3 31.1 %all-to-all-done = bf16[64,8,1344]{2,1,0:T(8,128)(2,1)S(1)} async-done(((bf16[64,8,1344]{2,1,0:T(8,128)(2,1)}), bf16[64,8,1344]{2,1,0:T(8,128)(2,1)S(1)}, u32[]{:S(2)}, u32[]{:S(2)}) %all-to-all-start) | async-done | bytes 1376288 | tf_op jit(solution)/shard_map/all_to_all | solution.py:21
  62.4 0.1 slice.18
  62.4 1.4 fusion.1
  63.9 6.1 %collective-permute-start = (f32[576,384]{1,0:T(8,128)}, f32[576,384]{1,0:T(8,128)S(1)}, u32[]{:S(2)}, u32[]{:S(2)}) collective-permute-start(f32[576,384]{1,0:T(8,128)} %fusion.1), channel_id=1, source_target_pairs={{0,1},{1,0},{2,3},{3,2},{4,5},{5,4},{6,7},{7,6},{8,9},{9,8},{10,11... | collective-permute-start | bytes 2654216 | tf_op jit(solution)/shard_map/ppermute | solution.py:149
  70.0 0.5 fusion.3
  70.5 1.7 %collective-permute-done = f32[576,384]{1,0:T(8,128)S(1)} collective-permute-done((f32[576,384]{1,0:T(8,128)}, f32[576,384]{1,0:T(8,128)S(1)}, u32[]{:S(2)}, u32[]{:S(2)}) %collective-permute-start) | collective-permute-done | bytes 884768 | tf_op jit(solution)/shard_map/ppermute | solution.py:149
  72.2 0.1 abs_reduce_fusion
  72.3 0.1 multiply_convert_fusion
  72.4 0.1 pad_maximum_fusion
  72.6 22.2 %all_to_all.20 = f16[8,80,384]{2,1,0:T(8,128)(2,1)S(1)} all-to-all(f16[8,80,384]{2,1,0:T(8,128)(2,1)S(1)} %pad_maximum_fusion), channel_id=1, replica_groups=mesh['y1'=2,'y0'=2,'z2'=2,'z1'=2,'z0'=2,'y2'=2,'x2'=2,'x1'=2,'x0'=2,'c'=..., dimensions={0} | all-to-all | bytes 983040 | tf_op jit(solution)/shard_map/all_to_all | solution.py:21
  94.8 0.1 multiply_reduce_fusion
  94.9 0.1 divide_convert_fusion
  95.0 15.5 %all_to_all.21 = bf16[8,72,384]{2,1,0:T(8,128)(2,1)S(1)} all-to-all(bf16[8,72,384]{2,1,0:T(8,128)(2,1)S(1)} %broadcast_in_dim.8), channel_id=1, replica_groups=mesh['y1'=2,'y0'=2,'z2'=2,'z1'=2,'z0'=2,'y2'=2,'x2'=2,'x1'=2,'x0'=2,'c'=..., dimensions={0} | all-to-all | bytes 884736 | tf_op jit(solution)/shard_map/all_to_all | solution.py:21
  110.6 5.5 %collective-permute-start.1 = (bf16[576,384]{1,0:T(8,128)(2,1)S(1)}, bf16[576,384]{1,0:T(8,128)(2,1)S(1)}, u32[]{:S(2)}, u32[]{:S(2)}) collective-permute-start(bf16[576,384]{1,0:T(8,128)(2,1)S(1)} %bitcast.18), channel_id=1, source_target_pairs={{0,1},{1,0},{2,3},{3,2},{4,5},{5,4},{6,7},{7,6},{8,9},{9,8},{10,11... | collective-permute-start | bytes 1327112 | tf_op jit(solution)/shard_map/ppermute | solution.py:159
  116.0 0.5 fusion.7
  116.5 0.9 collective-permute-done.1
  117.4 0.5 fusion
  117.9 0.3 copy.12
  118.2 26.4 %all_to_all.22.in_ref = bf16[64,8,576]{2,1,0:T(8,128)(2,1)S(1)} all-to-all(bf16[64,8,576]{2,1,0:T(8,128)(2,1)S(1)} %bitcast.17), channel_id=1, replica_groups=mesh['y1'=2,'y0'=2,'z2'=2,'z1'=2,'z0'=2,'y2'=2,'x2'=2,'x1'=2,'x0'=2,'c'=..., dimensions={0} | all-to-all | bytes 1179648 | tf_op jit(solution)/shard_map/all_to_all | solution.py:21
  144.6 2.0 %shard_map.56 = f32[10,8,3072]{2,1,0:T(8,128)} custom-call(s32[3]{0:T(128)} %left_ref.3, bf16[64,8,576]{2,1,0:T(8,128)(2,1)S(1)} %all_to_all.22.in_ref), custom_call_target="tpu_custom_call" | custom-call | tf_op jit(solution)/shard_map/pallas_call | solution.py:86
  (7 shorter events, 0.1 us)
Async XLA Ops:
  3.6 25.6 %copy-start = (f32[10]{0:T(128)S(1)}, f32[10]{0:T(128)}, u32[]{:S(2)}) copy-start(f32[10]{0:T(128)} %param.6) | copy-start | bytes 124
  3.6 26.2 %copy-start.1 = (s32[3]{0:T(128)S(1)}, s32[3]{0:T(128)}, u32[]{:S(2)}) copy-start(s32[3]{0:T(128)} %left_ref.3) | copy-start | bytes 40
  3.6 58.8 %all-to-all-start = ((bf16[64,8,1344]{2,1,0:T(8,128)(2,1)}), bf16[64,8,1344]{2,1,0:T(8,128)(2,1)S(1)}, u32[]{:S(2)}, u32[]{:S(2)}) async-start(bf16[64,8,1344]{2,1,0:T(8,128)(2,1)} %shard_map.55), calls=%async_computation | async-start | bytes 2883584 | tf_op jit(solution)/shard_map/all_to_all | solution.py:21
  63.9 8.4 %collective-permute-start = (f32[576,384]{1,0:T(8,128)}, f32[576,384]{1,0:T(8,128)S(1)}, u32[]{:S(2)}, u32[]{:S(2)}) collective-permute-start(f32[576,384]{1,0:T(8,128)} %fusion.1), channel_id=1, source_target_pairs={{0,1},{1,0},{2,3},{3,2},{4,5},{5,4},{6,7},{7,6},{8,9},{9,8},{10,11... | collective-permute-start | bytes 2654216 | tf_op jit(solution)/shard_map/ppermute | solution.py:149
  110.6 6.9 %collective-permute-start.1 = (bf16[576,384]{1,0:T(8,128)(2,1)S(1)}, bf16[576,384]{1,0:T(8,128)(2,1)S(1)}, u32[]{:S(2)}, u32[]{:S(2)}) collective-permute-start(bf16[576,384]{1,0:T(8,128)(2,1)S(1)} %bitcast.18), channel_id=1, source_target_pairs={{0,1},{1,0},{2,3},{3,2},{4,5},{5,4},{6,7},{7,6},{8,9},{9,8},{10,11... | collective-permute-start | bytes 1327112 | tf_op jit(solution)/shard_map/ppermute | solution.py:159

commit v10 on v9

--- a/solution.py
+++ b/solution.py
@@ -9,8 +9,8 @@
 GRP_BITS = ("y1", "y0", "z2", "z1", "z0")
 INNER_BITS = ("y2", "x2", "x1", "x0", "c")
 ALL_BITS = GRP_BITS + INNER_BITS
-A_BITS = ("y2", "y1", "y0", "z2")
-B_BITS = ("z1", "z0")
+A_BITS = ("y2", "z2", "y1", "z1")
+B_BITS = ("y0", "z0")
 AB_BITS = A_BITS + B_BITS
 B_SUM_BITS = ("c",)
 A_SUM_BITS = ("x2", "x1", "x0")

time: 150 us -> 155 us (1.033); the launches traced: 147 us -> 153 us
  blocking collectives: 64.1 us -> 69.3 us
  waiting for transfers between devices: 33.7 us -> 38.3 us
  starting transfers between devices: 35.5 us -> 32.5 us
    all_to_all x3, blocking collectives: 64.1 us -> 69.3 us  [exchange(): return lax.all_to_all(x, axes, split_axis=0, concat_axis=0, tiled=True)]
    all_to_all x1, waiting for transfers between devices: 31.1 us -> 35.6 us  [exchange(): return lax.all_to_all(x, axes, split_axis=0, concat_axis=0, tiled=True)]
    ppermute x1, starting transfers between devices: 6.1 us -> 3.06 us  [body(): received = lax.ppermute(partial_of(1 - b_sub), B_SUM_BITS, swap)]
where the time goes in v10:
time: 155 us; the launch traced here: 153 us
  blocking collectives  69.3 us (45%)
  waiting for transfers between devices  38.3 us (25%)
  starting transfers between devices  32.5 us (21%)
  Pallas kernels  4.91 us (3%)
  local copies, waits for them, and re-layouts  3.35 us (2%)
  matrix products  2.93 us (2%)
    all_to_all x3, blocking collectives, exchange(): return lax.all_to_all(x, axes, split_axis=0, concat_axis=0, tiled=True)  69.3 us
    all_to_all x1, waiting for transfers between devices, exchange(): return lax.all_to_all(x, axes, split_axis=0, concat_axis=0, tiled=True)  35.6 us
    all_to_all x1, starting transfers between devices, exchange(): return lax.all_to_all(x, axes, split_axis=0, concat_axis=0, tiled=True)  24 us
    ppermute x1, starting transfers between devices, body(): other_amps = lax.ppermute(amps, B_SUM_BITS, swap)  5.46 us
  transfers between devices with their start and end apart: 3, of which 3 were waited for; matrix products, arithmetic and copies ran while one was open for 3% of the time, Pallas kernels for 0%

profile of v10, /device:TPU:1, one launch (start us, length us, event | category | flops | bytes accessed | tf_op | source)
XLA Modules:
  0.0 153.3 jit_solution(9971747115874257938)
XLA Ops:
  0.7 2.9 %shard_map.55 = bf16[64,8,1344]{2,1,0:T(8,128)(2,1)} custom-call(s32[3]{0:T(128)} %left_ref.3, s32[1]{0:T(128)} %copy.15.right_ref, bf16[10,8,3072]{2,1,0:T(8,128)(2,1)} %b_ref.1), custom_call_target="tpu_custom_call" | custom-call | tf_op jit(solution)/shard_map/pallas_call | solution.py:48
  3.6 0.0 copy-start
  3.6 0.0 copy-start.1
  3.6 24.0 %all-to-all-start = ((bf16[64,8,1344]{2,1,0:T(8,128)(2,1)}), bf16[64,8,1344]{2,1,0:T(8,128)(2,1)S(1)}, u32[]{:S(2)}, u32[]{:S(2)}) async-start(bf16[64,8,1344]{2,1,0:T(8,128)(2,1)} %shard_map.55), calls=%async_computation | async-start | bytes 2883584 | tf_op jit(solution)/shard_map/all_to_all | solution.py:21
  27.6 0.8 dynamic_slice.21
  28.4 0.8 dynamic_slice.23
  29.2 0.0 copy-done
  29.2 0.6 dynamic_slice.20
  29.8 0.0 copy-done.1
  29.8 0.6 gather_fusion
  30.4 0.6 broadcast_add_fusion
  31.1 0.1 broadcast_subtract_fusion
  31.1 0.1 sub.51
  31.2 0.1 dynamic_slice.22
  31.3 35.6 %all-to-all-done = bf16[64,8,1344]{2,1,0:T(8,128)(2,1)S(1)} async-done(((bf16[64,8,1344]{2,1,0:T(8,128)(2,1)}), bf16[64,8,1344]{2,1,0:T(8,128)(2,1)S(1)}, u32[]{:S(2)}, u32[]{:S(2)}) %all-to-all-start) | async-done | bytes 1376288 | tf_op jit(solution)/shard_map/all_to_all | solution.py:21
  66.9 0.1 slice.18
  67.0 1.4 fusion.1
  68.4 3.1 %collective-permute-start = (f32[576,384]{1,0:T(8,128)}, f32[576,384]{1,0:T(8,128)S(1)}, u32[]{:S(2)}, u32[]{:S(2)}) collective-permute-start(f32[576,384]{1,0:T(8,128)} %fusion.1), channel_id=1, source_target_pairs={{0,1},{1,0},{2,3},{3,2},{4,5},{5,4},{6,7},{7,6},{8,9},{9,8},{10,11... | collective-permute-start | bytes 2654216 | tf_op jit(solution)/shard_map/ppermute | solution.py:149
  71.5 0.5 fusion.3
  72.0 1.7 %collective-permute-done = f32[576,384]{1,0:T(8,128)S(1)} collective-permute-done((f32[576,384]{1,0:T(8,128)}, f32[576,384]{1,0:T(8,128)S(1)}, u32[]{:S(2)}, u32[]{:S(2)}) %collective-permute-start) | collective-permute-done | bytes 884768 | tf_op jit(solution)/shard_map/ppermute | solution.py:149
  73.7 0.1 abs_reduce_fusion
  73.9 0.1 multiply_convert_fusion
  74.0 0.1 pad_maximum_fusion
  74.1 22.2 %all_to_all.20 = f16[8,80,384]{2,1,0:T(8,128)(2,1)S(1)} all-to-all(f16[8,80,384]{2,1,0:T(8,128)(2,1)S(1)} %pad_maximum_fusion), channel_id=1, replica_groups=mesh['y1'=2,'y0'=2,'z2'=2,'z1'=2,'z0'=2,'y2'=2,'x2'=2,'x1'=2,'x0'=2,'c'=..., dimensions={0} | all-to-all | bytes 983040 | tf_op jit(solution)/shard_map/all_to_all | solution.py:21
  96.3 0.1 multiply_reduce_fusion
  96.4 0.1 divide_convert_fusion
  96.6 15.5 %all_to_all.21 = bf16[8,72,384]{2,1,0:T(8,128)(2,1)S(1)} all-to-all(bf16[8,72,384]{2,1,0:T(8,128)(2,1)S(1)} %broadcast_in_dim.8), channel_id=1, replica_groups=mesh['y1'=2,'y0'=2,'z2'=2,'z1'=2,'z0'=2,'y2'=2,'x2'=2,'x1'=2,'x0'=2,'c'=..., dimensions={0} | all-to-all | bytes 884736 | tf_op jit(solution)/shard_map/all_to_all | solution.py:21
  112.1 5.5 %collective-permute-start.1 = (bf16[576,384]{1,0:T(8,128)(2,1)S(1)}, bf16[576,384]{1,0:T(8,128)(2,1)S(1)}, u32[]{:S(2)}, u32[]{:S(2)}) collective-permute-start(bf16[576,384]{1,0:T(8,128)(2,1)S(1)} %bitcast.18), channel_id=1, source_target_pairs={{0,1},{1,0},{2,3},{3,2},{4,5},{5,4},{6,7},{7,6},{8,9},{9,8},{10,11... | collective-permute-start | bytes 1327112 | tf_op jit(solution)/shard_map/ppermute | solution.py:159
  117.6 0.5 fusion.7
  118.1 0.9 collective-permute-done.1
  119.0 0.5 fusion
  119.5 0.3 copy.12
  119.8 31.6 %all_to_all.22.in_ref = bf16[64,8,576]{2,1,0:T(8,128)(2,1)S(1)} all-to-all(bf16[64,8,576]{2,1,0:T(8,128)(2,1)S(1)} %bitcast.17), channel_id=1, replica_groups=mesh['y1'=2,'y0'=2,'z2'=2,'z1'=2,'z0'=2,'y2'=2,'x2'=2,'x1'=2,'x0'=2,'c'=..., dimensions={0} | all-to-all | bytes 1179648 | tf_op jit(solution)/shard_map/all_to_all | solution.py:21
  151.3 2.0 %shard_map.56 = f32[10,8,3072]{2,1,0:T(8,128)} custom-call(s32[3]{0:T(128)} %left_ref.3, bf16[64,8,576]{2,1,0:T(8,128)(2,1)S(1)} %all_to_all.22.in_ref), custom_call_target="tpu_custom_call" | custom-call | tf_op jit(solution)/shard_map/pallas_call | solution.py:86
  (7 shorter events, 0.1 us)
Async XLA Ops:
  3.6 25.6 %copy-start = (f32[10]{0:T(128)S(1)}, f32[10]{0:T(128)}, u32[]{:S(2)}) copy-start(f32[10]{0:T(128)} %param.6) | copy-start | bytes 124
  3.6 26.2 %copy-start.1 = (s32[3]{0:T(128)S(1)}, s32[3]{0:T(128)}, u32[]{:S(2)}) copy-start(s32[3]{0:T(128)} %left_ref.3) | copy-start | bytes 40
  3.6 63.3 %all-to-all-start = ((bf16[64,8,1344]{2,1,0:T(8,128)(2,1)}), bf16[64,8,1344]{2,1,0:T(8,128)(2,1)S(1)}, u32[]{:S(2)}, u32[]{:S(2)}) async-start(bf16[64,8,1344]{2,1,0:T(8,128)(2,1)} %shard_map.55), calls=%async_computation | async-start | bytes 2883584 | tf_op jit(solution)/shard_map/all_to_all | solution.py:21
  68.4 5.3 %collective-permute-start = (f32[576,384]{1,0:T(8,128)}, f32[576,384]{1,0:T(8,128)S(1)}, u32[]{:S(2)}, u32[]{:S(2)}) collective-permute-start(f32[576,384]{1,0:T(8,128)} %fusion.1), channel_id=1, source_target_pairs={{0,1},{1,0},{2,3},{3,2},{4,5},{5,4},{6,7},{7,6},{8,9},{9,8},{10,11... | collective-permute-start | bytes 2654216 | tf_op jit(solution)/shard_map/ppermute | solution.py:149
  112.1 6.9 %collective-permute-start.1 = (bf16[576,384]{1,0:T(8,128)(2,1)S(1)}, bf16[576,384]{1,0:T(8,128)(2,1)S(1)}, u32[]{:S(2)}, u32[]{:S(2)}) collective-permute-start(bf16[576,384]{1,0:T(8,128)(2,1)S(1)} %bitcast.18), channel_id=1, source_target_pairs={{0,1},{1,0},{2,3},{3,2},{4,5},{5,4},{6,7},{7,6},{8,9},{9,8},{10,11... | collective-permute-start | bytes 1327112 | tf_op jit(solution)/shard_map/ppermute | solution.py:159

commit v11 on v10

--- a/solution.py
+++ b/solution.py
@@ -9,8 +9,8 @@
 GRP_BITS = ("y1", "y0", "z2", "z1", "z0")
 INNER_BITS = ("y2", "x2", "x1", "x0", "c")
 ALL_BITS = GRP_BITS + INNER_BITS
-A_BITS = ("y2", "z2", "y1", "z1")
-B_BITS = ("y0", "z0")
+A_BITS = ("z2", "z1", "z0", "y2")
+B_BITS = ("y1", "y0")
 AB_BITS = A_BITS + B_BITS
 B_SUM_BITS = ("c",)
 A_SUM_BITS = ("x2", "x1", "x0")

time: 155 us -> 149 us (0.961)
  blocking collectives: 69.3 us -> 64.1 us
  waiting for transfers between devices: 38.3 us -> 34.9 us
  starting transfers between devices: 32.5 us -> 34.7 us
    all_to_all x3, blocking collectives: 69.3 us -> 64.1 us  [exchange(): return lax.all_to_all(x, axes, split_axis=0, concat_axis=0, tiled=True)]
    all_to_all x1, waiting for transfers between devices: 35.6 us -> 32.3 us  [exchange(): return lax.all_to_all(x, axes, split_axis=0, concat_axis=0, tiled=True)]
    ppermute x1, starting transfers between devices: 3.06 us -> 5.29 us  [body(): received = lax.ppermute(partial_of(1 - b_sub), B_SUM_BITS, swap)]
where the time goes in v11:
time: 149 us; the launch traced here: 147 us
  blocking collectives  64.1 us (43%)
  waiting for transfers between devices  34.9 us (23%)
  starting transfers between devices  34.7 us (23%)
  Pallas kernels  4.91 us (3%)
  local copies, waits for them, and re-layouts  3.35 us (2%)
  matrix products  2.93 us (2%)
    all_to_all x3, blocking collectives, exchange(): return lax.all_to_all(x, axes, split_axis=0, concat_axis=0, tiled=True)  64.1 us
    all_to_all x1, waiting for transfers between devices, exchange(): return lax.all_to_all(x, axes, split_axis=0, concat_axis=0, tiled=True)  32.3 us
    all_to_all x1, starting transfers between devices, exchange(): return lax.all_to_all(x, axes, split_axis=0, concat_axis=0, tiled=True)  24 us
    ppermute x1, starting transfers between devices, body(): other_amps = lax.ppermute(amps, B_SUM_BITS, swap)  5.46 us
    ppermute x1, starting transfers between devices, body(): received = lax.ppermute(partial_of(1 - b_sub), B_SUM_BITS, swap)  5.29 us
  transfers between devices with their start and end apart: 3, of which 3 were waited for; matrix products, arithmetic and copies ran while one was open for 3% of the time, Pallas kernels for 0%

profile of v11, /device:TPU:1, one launch (start us, length us, event | category | flops | bytes accessed | tf_op | source)
XLA Modules:
  0.0 147.0 jit_solution(16521930806086654273)
XLA Ops:
  0.7 2.9 %shard_map.55 = bf16[64,8,1344]{2,1,0:T(8,128)(2,1)} custom-call(s32[3]{0:T(128)} %left_ref.3, s32[1]{0:T(128)} %copy.15.right_ref, bf16[10,8,3072]{2,1,0:T(8,128)(2,1)} %b_ref.1), custom_call_target="tpu_custom_call" | custom-call | tf_op jit(solution)/shard_map/pallas_call | solution.py:48
  3.6 0.0 copy-start
  3.6 0.0 copy-start.1
  3.6 24.0 %all-to-all-start = ((bf16[64,8,1344]{2,1,0:T(8,128)(2,1)}), bf16[64,8,1344]{2,1,0:T(8,128)(2,1)S(1)}, u32[]{:S(2)}, u32[]{:S(2)}) async-start(bf16[64,8,1344]{2,1,0:T(8,128)(2,1)} %shard_map.55), calls=%async_computation | async-start | bytes 2883584 | tf_op jit(solution)/shard_map/all_to_all | solution.py:21
  27.6 0.8 dynamic_slice.21
  28.4 0.8 dynamic_slice.23
  29.2 0.0 copy-done
  29.2 0.6 dynamic_slice.20
  29.8 0.0 copy-done.1
  29.8 0.6 gather_fusion
  30.4 0.6 broadcast_add_fusion
  31.1 0.1 broadcast_subtract_fusion
  31.1 0.1 sub.51
  31.2 0.1 dynamic_slice.22
  31.3 32.3 %all-to-all-done = bf16[64,8,1344]{2,1,0:T(8,128)(2,1)S(1)} async-done(((bf16[64,8,1344]{2,1,0:T(8,128)(2,1)}), bf16[64,8,1344]{2,1,0:T(8,128)(2,1)S(1)}, u32[]{:S(2)}, u32[]{:S(2)}) %all-to-all-start) | async-done | bytes 1376288 | tf_op jit(solution)/shard_map/all_to_all | solution.py:21
  63.6 0.1 slice.18
  63.7 1.4 fusion.1
  65.1 5.3 %collective-permute-start = (f32[576,384]{1,0:T(8,128)}, f32[576,384]{1,0:T(8,128)S(1)}, u32[]{:S(2)}, u32[]{:S(2)}) collective-permute-start(f32[576,384]{1,0:T(8,128)} %fusion.1), channel_id=1, source_target_pairs={{0,1},{1,0},{2,3},{3,2},{4,5},{5,4},{6,7},{7,6},{8,9},{9,8},{10,11... | collective-permute-start | bytes 2654216 | tf_op jit(solution)/shard_map/ppermute | solution.py:149
  70.4 0.5 fusion.3
  70.9 1.7 %collective-permute-done = f32[576,384]{1,0:T(8,128)S(1)} collective-permute-done((f32[576,384]{1,0:T(8,128)}, f32[576,384]{1,0:T(8,128)S(1)}, u32[]{:S(2)}, u32[]{:S(2)}) %collective-permute-start) | collective-permute-done | bytes 884768 | tf_op jit(solution)/shard_map/ppermute | solution.py:149
  72.6 0.1 abs_reduce_fusion
  72.8 0.1 multiply_convert_fusion
  72.9 0.1 pad_maximum_fusion
  73.0 22.2 %all_to_all.20 = f16[8,80,384]{2,1,0:T(8,128)(2,1)S(1)} all-to-all(f16[8,80,384]{2,1,0:T(8,128)(2,1)S(1)} %pad_maximum_fusion), channel_id=1, replica_groups=mesh['y1'=2,'y0'=2,'z2'=2,'z1'=2,'z0'=2,'y2'=2,'x2'=2,'x1'=2,'x0'=2,'c'=..., dimensions={0} | all-to-all | bytes 983040 | tf_op jit(solution)/shard_map/all_to_all | solution.py:21
  95.2 0.1 multiply_reduce_fusion
  95.3 0.1 divide_convert_fusion
  95.5 15.5 %all_to_all.21 = bf16[8,72,384]{2,1,0:T(8,128)(2,1)S(1)} all-to-all(bf16[8,72,384]{2,1,0:T(8,128)(2,1)S(1)} %broadcast_in_dim.8), channel_id=1, replica_groups=mesh['y1'=2,'y0'=2,'z2'=2,'z1'=2,'z0'=2,'y2'=2,'x2'=2,'x1'=2,'x0'=2,'c'=..., dimensions={0} | all-to-all | bytes 884736 | tf_op jit(solution)/shard_map/all_to_all | solution.py:21
  111.0 5.5 %collective-permute-start.1 = (bf16[576,384]{1,0:T(8,128)(2,1)S(1)}, bf16[576,384]{1,0:T(8,128)(2,1)S(1)}, u32[]{:S(2)}, u32[]{:S(2)}) collective-permute-start(bf16[576,384]{1,0:T(8,128)(2,1)S(1)} %bitcast.18), channel_id=1, source_target_pairs={{0,1},{1,0},{2,3},{3,2},{4,5},{5,4},{6,7},{7,6},{8,9},{9,8},{10,11... | collective-permute-start | bytes 1327112 | tf_op jit(solution)/shard_map/ppermute | solution.py:159
  116.5 0.5 fusion.7
  117.0 0.9 collective-permute-done.1
  117.9 0.5 fusion
  118.4 0.3 copy.12
  118.7 26.4 %all_to_all.22.in_ref = bf16[64,8,576]{2,1,0:T(8,128)(2,1)S(1)} all-to-all(bf16[64,8,576]{2,1,0:T(8,128)(2,1)S(1)} %bitcast.17), channel_id=1, replica_groups=mesh['y1'=2,'y0'=2,'z2'=2,'z1'=2,'z0'=2,'y2'=2,'x2'=2,'x1'=2,'x0'=2,'c'=..., dimensions={0} | all-to-all | bytes 1179648 | tf_op jit(solution)/shard_map/all_to_all | solution.py:21
  145.0 2.0 %shard_map.56 = f32[10,8,3072]{2,1,0:T(8,128)} custom-call(s32[3]{0:T(128)} %left_ref.3, bf16[64,8,576]{2,1,0:T(8,128)(2,1)S(1)} %all_to_all.22.in_ref), custom_call_target="tpu_custom_call" | custom-call | tf_op jit(solution)/shard_map/pallas_call | solution.py:86
  (7 shorter events, 0.1 us)
Async XLA Ops:
  3.6 25.6 %copy-start = (f32[10]{0:T(128)S(1)}, f32[10]{0:T(128)}, u32[]{:S(2)}) copy-start(f32[10]{0:T(128)} %param.6) | copy-start | bytes 124
  3.6 26.2 %copy-start.1 = (s32[3]{0:T(128)S(1)}, s32[3]{0:T(128)}, u32[]{:S(2)}) copy-start(s32[3]{0:T(128)} %left_ref.3) | copy-start | bytes 40
  3.6 60.0 %all-to-all-start = ((bf16[64,8,1344]{2,1,0:T(8,128)(2,1)}), bf16[64,8,1344]{2,1,0:T(8,128)(2,1)S(1)}, u32[]{:S(2)}, u32[]{:S(2)}) async-start(bf16[64,8,1344]{2,1,0:T(8,128)(2,1)} %shard_map.55), calls=%async_computation | async-start | bytes 2883584 | tf_op jit(solution)/shard_map/all_to_all | solution.py:21
  65.1 7.5 %collective-permute-start = (f32[576,384]{1,0:T(8,128)}, f32[576,384]{1,0:T(8,128)S(1)}, u32[]{:S(2)}, u32[]{:S(2)}) collective-permute-start(f32[576,384]{1,0:T(8,128)} %fusion.1), channel_id=1, source_target_pairs={{0,1},{1,0},{2,3},{3,2},{4,5},{5,4},{6,7},{7,6},{8,9},{9,8},{10,11... | collective-permute-start | bytes 2654216 | tf_op jit(solution)/shard_map/ppermute | solution.py:149
  111.0 6.9 %collective-permute-start.1 = (bf16[576,384]{1,0:T(8,128)(2,1)S(1)}, bf16[576,384]{1,0:T(8,128)(2,1)S(1)}, u32[]{:S(2)}, u32[]{:S(2)}) collective-permute-start(bf16[576,384]{1,0:T(8,128)(2,1)S(1)} %bitcast.18), channel_id=1, source_target_pairs={{0,1},{1,0},{2,3},{3,2},{4,5},{5,4},{6,7},{7,6},{8,9},{9,8},{10,11... | collective-permute-start | bytes 1327112 | tf_op jit(solution)/shard_map/ppermute | solution.py:159
